TPU v7x, 256 devices: a whole 4x4x8 slice. The times are simulated.
256 devices in a mesh: lat: 16 (over z, core), lon: 16 (over y, x).
Axes of the slice: x: 4, y: 4, z: 8, core: 2. Of those that a mesh axis runs over, the one named last changes fastest.
Arguments:
- density: float32 [75, 256, 4096], P(None, 'lat', 'lon'), may hold values from -24 to 24
- tend_east: float32 [75, 256, 4096], P(None, 'lat', 'lon'), may hold values from -6 to 6
- tend_north: float32 [75, 256, 4096], P(None, 'lat', 'lon'), may hold values from -6 to 6
- thickness: float32 [75], replicated, may hold values from 0.02 to 0.2
- levels: int32 [256, 4096], P('lat', 'lon'), may hold values from 1 to 75
- ocean_mask: int32 [256, 4096], P('lat', 'lon'), may hold values 0 or 1
- eta_prev: float32 [256, 4096], P('lat', 'lon'), may hold values from -1.2 to 1.2
- coarse: float32 [4096, 4096], P(('lat', 'lon')), as said below
Outputs:
- surface: float32 [256, 4096], P('lat', 'lon')
- precond_residual: float32 [256, 4096], P('lat', 'lon')
Inputs may be any that keep to these rules, and one draw needn't show every extreme that they name: coarse is symmetric positive definite.
All inputs are finite; a program needn't handle non-finite values. No bound on the sum of `ocean_mask` on one device may be relied on, other than what follows from the above.
Results may differ from a plain program's by a relative error of at most 0.0003.
Values sent between devices are 32-bit elements; how exact they have to be, the bound alone decides.
No kernel may reach another device: no remote copies, remote signals or barrier semaphores. Data moves between devices by JAX's collectives and lax.ppermute only.
A program may use at most 64 MiB of HBM per device.

v0:
```python
import jax
import jax.numpy as jnp
from jax import lax
from jax.sharding import PartitionSpec as P

K = 75
TILE_SIDE = 4
ITERS = 2


surface_coeff = 0.25
highest = lax.Precision.HIGHEST


def with_halo(shard, sides, width):
    for axis, dim in sides:
        peers, length = (lax.axis_size(axis), shard.shape[dim])
        up = [(i, (i + 1) % peers) for i in range(peers)]
        down = [(j, i) for i, j in up]
        last = lax.slice_in_dim(shard, length - width, length, axis=dim)
        leading = lax.slice_in_dim(shard, 0, width, axis=dim)
        before = lax.ppermute(last, axis, up)
        after = lax.ppermute(leading, axis, down)
        shard = jnp.concatenate([before, shard, after], axis=dim)
    return shard


def wall_rows(framed, rim_width):
    row_count = framed.shape[1]
    row_index = lax.broadcasted_iota(jnp.int32, (1, row_count, 1), 1)
    position = lax.axis_index("lat")
    last_index = lax.axis_size("lat") - 1
    southern = jnp.logical_and(position == 0, row_index < rim_width)
    northern = jnp.logical_and(position == last_index, row_index >= row_count - rim_width)
    return jnp.where(jnp.logical_or(southern, northern), 0.0, framed)


def plane_halo(planes):
    return wall_rows(with_halo(planes, (("lat", 1), ("lon", 2)), 1), 1)


def global_sum(partial_value):
    return lax.psum(partial_value, ("lat", "lon"))


def gather_coarse(own_values):
    return lax.all_gather(own_values, ("lat", "lon"), axis=0, tiled=True)


def restrict_local(values, ocean_share):
    tile_rows = values.shape[0] // TILE_SIDE
    tile_cols = values.shape[1] // TILE_SIDE
    tiled_sum = (values * ocean_share).reshape(TILE_SIDE, tile_rows, TILE_SIDE, tile_cols)
    return jnp.sum(tiled_sum, axis=(1, 3)).reshape(-1)


def prolong_local(coarse_values, ocean_share):
    tile_rows = ocean_share.shape[0] // TILE_SIDE
    tile_cols = ocean_share.shape[1] // TILE_SIDE
    blocks = coarse_values.reshape(TILE_SIDE, 1, TILE_SIDE, 1)
    spread = jnp.broadcast_to(blocks, (TILE_SIDE, tile_rows, TILE_SIDE, tile_cols))
    return spread.reshape(ocean_share.shape) * ocean_share


def east_fourth(own_rows):
    return (
        8.0 * (own_rows[:, :, 3:-1] - own_rows[:, :, 1:-3])
        - (own_rows[:, :, 4:] - own_rows[:, :, :-4])
    ) / 12.0


def north_fourth(own_cols):
    return (
        8.0 * (own_cols[:, 3:-1, :] - own_cols[:, 1:-3, :])
        - (own_cols[:, 4:, :] - own_cols[:, :-4, :])
    ) / 12.0


def apply_operator(face_list, diagonal, values, beside_all):
    east_face, west_face, north_face, south_face = face_list
    return diagonal * values - (
        east_face * beside_all[1:-1, 2:]
        + west_face * beside_all[1:-1, :-2]
        + north_face * beside_all[2:, 1:-1]
        + south_face * beside_all[:-2, 1:-1]
    )


def body(density, tend_east, tend_north, thickness, levels, ocean_mask, eta_prev, coarse):
    wet_levels = levels * ocean_mask
    ocean_share = ocean_mask.astype(jnp.float32)
    layer_weight = thickness[:, None, None]
    depth_index = lax.broadcasted_iota(jnp.int32, (K,) + wet_levels.shape, 0)
    active = (depth_index < wet_levels[None]).astype(jnp.float32)
    lower_ones = (
        lax.broadcasted_iota(jnp.int32, (K, K), 1) <= lax.broadcasted_iota(jnp.int32, (K, K), 0)
    ).astype(jnp.float32)
    pressure = (
        jnp.einsum("kj,jab->kab", lower_ones, layer_weight * density, precision=highest) * active
    )
    solution = ocean_share * eta_prev
    framed = wall_rows(with_halo(pressure, (("lat", 1), ("lon", 2)), 2), 2)
    east_diff = east_fourth(framed[:, 2:-2, :])
    north_diff = north_fourth(framed[:, :, 2:-2])
    force_east = jnp.sum(layer_weight * active * (tend_east - east_diff), axis=0)
    force_north = jnp.sum(layer_weight * active * (tend_north - north_diff), axis=0)
    column_depth = jnp.sum(layer_weight * active, axis=0)
    planes = plane_halo(jnp.stack([force_east, force_north, column_depth, solution]))
    right_side = (
        ocean_share
        * 0.5
        * (planes[0, 1:-1, :-2] - planes[0, 1:-1, 2:] + planes[1, :-2, 1:-1] - planes[1, 2:, 1:-1])
    )
    depth_framed = planes[2]
    solution_framed = planes[3]
    center = depth_framed[1:-1, 1:-1]
    face_list = (
        jnp.minimum(center, depth_framed[1:-1, 2:]),
        jnp.minimum(center, depth_framed[1:-1, :-2]),
        jnp.minimum(center, depth_framed[2:, 1:-1]),
        jnp.minimum(center, depth_framed[:-2, 1:-1]),
    )
    diagonal = ocean_share * (
        surface_coeff + face_list[0] + face_list[1] + face_list[2] + face_list[3]
    ) + (1.0 - ocean_share)

    def precondition(values):
        coarse_all = gather_coarse(restrict_local(values, ocean_share))
        return values / diagonal + prolong_local(
            jnp.dot(coarse, coarse_all, precision=highest), ocean_share
        )

    residual = right_side - apply_operator(face_list, diagonal, solution, solution_framed)
    precond = precondition(residual)
    direction = precond
    rz_now = global_sum(jnp.sum(residual * precond))
    for iteration in range(ITERS):
        beside_all = plane_halo(direction[None])[0]
        image_field = apply_operator(face_list, diagonal, direction, beside_all)
        step_length = rz_now / global_sum(jnp.sum(direction * image_field))
        solution = solution + step_length * direction
        residual = residual - step_length * image_field
        precond = precondition(residual)
        if iteration + 1 < ITERS:
            rz_next = global_sum(jnp.sum(residual * precond))
            direction = precond + rz_next / rz_now * direction
            rz_now = rz_next
    return (solution, precond)


def solution(mesh):
    return jax.shard_map(
        body,
        mesh=mesh,
        in_specs=(
            P(None, "lat", "lon"),
            P(None, "lat", "lon"),
            P(None, "lat", "lon"),
            P(),
            P("lat", "lon"),
            P("lat", "lon"),
            P("lat", "lon"),
            P(("lat", "lon"), None),
        ),
        out_specs=(P("lat", "lon"), P("lat", "lon")),
        check_vma=False,
    )
```

profile of v0, /device:TPU:1, one launch (start us, length us, event | category | flops | bytes accessed | tf_op | source)
XLA Modules:
  0.0 525.2 jit_solution(2610545018374523092)
XLA Ops:
  0.6 0.8 mul.159
  1.4 0.6 copy-done.5
  2.0 2.8 convolution_select_fusion
  4.9 3.0 collective-permute-start
  8.2 0.6 fusion.28
  8.8 1.4 collective-permute-done
  10.2 2.8 collective-permute-done.1
  13.1 0.3 fusion.34
  13.4 0.9 copy.25
  14.3 1.2 collective-permute-start.2
  15.5 0.3 copy.26
  15.8 3.8 collective-permute-start.3
  19.6 0.5 and_or_fusion
  20.2 0.5 collective-permute-done.2
  20.6 0.4 copy.27
  21.0 1.1 copy.28
  22.2 1.7 maximum_select_fusion
  23.9 2.6 fusion
  26.6 0.7 collective-permute-start.4
  27.3 2.1 collective-permute-start.5
  29.4 0.6 collective-permute-done.4
  30.0 0.3 collective-permute-done.5
  30.5 5.0 collective-permute-start.7
  35.5 1.4 collective-permute-done.6
  37.6 82.0 %all-reduce = f32[4096]{0:T(1024)S(1)} all-reduce(f32[4096]{0:T(1024)S(1)} %dynamic-update-slice), channel_id=1, replica_groups=mesh['lat'=16,'lon'=16] {'lat','lon'}, use_global_device_ids=true, to_apply=%add | all-reduce | flops 4096 | bytes 32768
  119.7 0.4 convolution_bitcast_fusion.2
  120.4 1.0 collective-permute-start.9
  121.4 0.6 collective-permute-done.8
  122.0 1.4 collective-permute-done.9
  123.5 4.8 collective-permute-start.11
  128.3 1.1 collective-permute-done.10
  129.5 0.7 multiply_reduce_fusion.2
  130.2 79.6 %all-reduce.3 = (f32[]{:T(128)}, f32[]{:T(128)}) all-reduce(f32[]{:T(128)} %get-tuple-element.6, f32[]{:T(128)} %get-tuple-element.5), channel_id=1, replica_groups=mesh['lat'=16,'lon'=16] {'lat','lon'}, use_global_device_ids=true, to_apply=%region_5.6 | all-reduce | flops 2 | bytes 16 | tf_op jit(solution)/shard_map/psum | solution.py:43
  211.6 72.8 %all-reduce.1 = f32[4096]{0:T(1024)S(1)} all-reduce(f32[4096]{0:T(1024)S(1)} %dynamic-update-slice.1), channel_id=1, replica_groups=mesh['lat'=16,'lon'=16] {'lat','lon'}, use_global_device_ids=true, to_apply=%add.1 | all-reduce | flops 4096 | bytes 32768
  284.4 0.4 convolution_bitcast_fusion.1
  285.1 0.6 multiply_reduce_fusion.1
  285.7 73.5 %psum.30 = f32[]{:T(128)} all-reduce(f32[]{:T(128)} %multiply_reduce_fusion.1), channel_id=1, replica_groups=mesh['lat'=16,'lon'=16] {'lat','lon'}, use_global_device_ids=true, to_apply=%region_10.11 | all-reduce | flops 1 | bytes 8 | tf_op jit(solution)/shard_map/psum | solution.py:43
  360.5 1.5 collective-permute-start.12
  362.0 0.7 collective-permute-done.12
  362.8 2.3 collective-permute-done.13
  365.1 0.7 collective-permute-start.14
  365.8 4.1 collective-permute-start.15
  369.9 1.1 collective-permute-done.14
  371.1 0.7 multiply_reduce_fusion
  371.8 77.7 %psum.31 = f32[]{:T(128)} all-reduce(f32[]{:T(128)} %get-tuple-element.9), channel_id=1, replica_groups=mesh['lat'=16,'lon'=16] {'lat','lon'}, use_global_device_ids=true, to_apply=%region_12.13 | all-reduce | flops 1 | bytes 8 | tf_op jit(solution)/shard_map/psum | solution.py:43
  451.3 72.6 %all-reduce.2 = f32[4096]{0:T(1024)S(1)} all-reduce(f32[4096]{0:T(1024)S(1)} %dynamic-update-slice.2), channel_id=1, replica_groups=mesh['lat'=16,'lon'=16] {'lat','lon'}, use_global_device_ids=true, to_apply=%add.2 | all-reduce | flops 4096 | bytes 32768
  523.9 0.4 convolution_bitcast_fusion
  524.5 0.6 multiply_add_fusion
  (73 shorter events, 3.5 us)
Async XLA Ops:
  0.6 119.0 %copy-start = (f32[16,4096]{1,0:T(8,128)S(1)}, f32[16,4096]{1,0:T(8,128)}, u32[]{:S(2)}) copy-start(f32[16,4096]{1,0:T(8,128)} %param.15) | copy-start | bytes 786436
  1.4 0.6 copy-start.5
  2.0 6.1 %copy-start.1 = (s32[16,256]{1,0:T(8,128)S(1)}, s32[16,256]{1,0:T(8,128)}, u32[]{:S(2)}) copy-start(s32[16,256]{1,0:T(8,128)} %param.13) | copy-start | bytes 49156
  2.0 6.1 %copy-start.7 = (f32[16,256]{1,0:T(8,128)S(1)}, f32[16,256]{1,0:T(8,128)}, u32[]{:S(2)}) copy-start(f32[16,256]{1,0:T(8,128)} %param.14) | copy-start | bytes 49156
  4.9 5.3 %collective-permute-start = (f32[75,2,256]{2,0,1:T(8,128)S(1)}, f32[75,2,256]{2,0,1:T(8,128)S(1)}, u32[]{:S(2)}, u32[]{:S(2)}) collective-permute-start(f32[75,2,256]{2,0,1:T(8,128)S(1)} %get-tuple-element.23), channel_id=1, source_target_pairs={{0,16},{16,32},{32,48},{48,64},{64,80},{80,96},{96,112},{112,128},... | collective-permute-start | bytes 460808 | tf_op jit(solution)/shard_map/ppermute | solution.py:22
  7.9 5.0 collective-permute-start.1
  14.3 6.3 %collective-permute-start.2 = (f32[75,20,2]{0,2,1:T(2,128)}, f32[75,20,2]{0,2,1:T(2,128)S(1)}, u32[]{:S(2)}, u32[]{:S(2)}) collective-permute-start(f32[75,20,2]{0,2,1:T(2,128)} %copy.25), channel_id=1, source_target_pairs={{0,1},{1,2},{2,3},{3,4},{4,5},{5,6},{6,7},{7,8},{8,9},{9,10},{10,1... | collective-permute-start | bytes 36008 | tf_op jit(solution)/shard_map/ppermute | solution.py:22
  15.8 5.2 collective-permute-start.3
  22.1 1.8 copy-start.2
  22.1 1.8 copy-start.3
  22.1 1.8 copy-start.6
  22.1 1.8 copy-start.9
  23.9 2.6 copy-start.4
  23.9 13.1 %copy-start.8 = (f32[16,256]{1,0:T(8,128)S(1)}, f32[16,256]{1,0:T(8,128)}, u32[]{:S(2)}) copy-start(f32[16,256]{1,0:T(8,128)} %param.14) | copy-start | bytes 49156
  26.6 3.4 collective-permute-start.4
  27.3 3.0 collective-permute-start.5
  30.4 6.4 %collective-permute-start.6 = (f32[4,18,1]{2,1,0:T(8,128)S(1)}, f32[4,18,1]{2,1,0:T(8,128)S(1)}, u32[]{:S(2)}, u32[]{:S(2)}) collective-permute-start(f32[4,18,1]{2,1,0:T(8,128)S(1)} %get-tuple-element.27), channel_id=1, source_target_pairs={{0,1},{1,2},{2,3},{3,4},{4,5},{5,6},{6,7},{7,8},{8,9},{9,10},{10,1... | collective-permute-start | bytes 872 | tf_op jit(solution)/shard_map/ppermute | solution.py:22
  30.5 6.4 %collective-permute-start.7 = (f32[4,18,1]{2,1,0:T(8,128)S(1)}, f32[4,18,1]{2,1,0:T(8,128)S(1)}, u32[]{:S(2)}, u32[]{:S(2)}) collective-permute-start(f32[4,18,1]{2,1,0:T(8,128)S(1)} %get-tuple-element.28), channel_id=1, source_target_pairs={{1,0},{2,1},{3,2},{4,3},{5,4},{6,5},{7,6},{8,7},{9,8},{10,9},{11,1... | collective-permute-start | bytes 872 | tf_op jit(solution)/shard_map/ppermute | solution.py:23
  120.4 1.7 collective-permute-start.8
  120.4 3.0 collective-permute-start.9
  123.5 5.9 %collective-permute-start.10 = (f32[1,18,1]{2,1,0:T(8,128)S(1)}, f32[1,18,1]{2,1,0:T(8,128)S(1)}, u32[]{:S(2)}, u32[]{:S(2)}) collective-permute-start(f32[1,18,1]{2,1,0:T(8,128)S(1)} %get-tuple-element.33), channel_id=1, source_target_pairs={{0,1},{1,2},{2,3},{3,4},{4,5},{5,6},{6,7},{7,8},{8,9},{9,10},{10,1... | collective-permute-start | bytes 224 | tf_op jit(solution)/shard_map/ppermute | solution.py:22
  123.5 5.9 %collective-permute-start.11 = (f32[1,18,1]{2,1,0:T(8,128)S(1)}, f32[1,18,1]{2,1,0:T(8,128)S(1)}, u32[]{:S(2)}, u32[]{:S(2)}) collective-permute-start(f32[1,18,1]{2,1,0:T(8,128)S(1)} %get-tuple-element.34), channel_id=1, source_target_pairs={{1,0},{2,1},{3,2},{4,3},{5,4},{6,5},{7,6},{8,7},{9,8},{10,9},{11,1... | collective-permute-start | bytes 224 | tf_op jit(solution)/shard_map/ppermute | solution.py:23
  360.5 2.3 collective-permute-start.12
  362.0 3.0 collective-permute-start.13
  365.1 5.9 %collective-permute-start.14 = (f32[1,18,1]{2,1,0:T(8,128)S(1)}, f32[1,18,1]{2,1,0:T(8,128)S(1)}, u32[]{:S(2)}, u32[]{:S(2)}) collective-permute-start(f32[1,18,1]{2,1,0:T(8,128)S(1)} %get-tuple-element.31), channel_id=1, source_target_pairs={{0,1},{1,2},{2,3},{3,4},{4,5},{5,6},{6,7},{7,8},{8,9},{9,10},{10,1... | collective-permute-start | bytes 224 | tf_op jit(solution)/shard_map/ppermute | solution.py:22
  365.8 5.2 collective-permute-start.15
where the time goes:
time: 527 us; the launch traced here: 525 us
  blocking collectives  458 us (87%)
  starting transfers between devices  28.2 us (5%)
  waiting for transfers between devices  14.2 us (3%)
  other arithmetic  9.79 us (2%)
  local copies, waits for them, and re-layouts  5.91 us (1%)
    psum x3, blocking collectives, global_sum(): return lax.psum(partial_value, ('lat', 'lon'))  231 us
    unnamed x3, blocking collectives  227 us
    ppermute x8, starting transfers between devices, with_halo(): after = lax.ppermute(leading, axis, down)  20.9 us
  transfers between devices with their start and end apart: 16, of which 12 were waited for; matrix products, arithmetic and copies ran while one was open for 0% of the time, Pallas kernels for 0%

commit v1 on v0

v1 whole, which is shorter than its diff:
```python
import jax
import jax.numpy as jnp
from jax import lax
from jax.experimental import pallas as pl
from jax.experimental.pallas import tpu as pltpu
from jax.sharding import PartitionSpec as P

K = 75
KB = 15
R = 16
L = 256
H = 128
NLON = 16
NLAT = 16
NDEV = 256
EPS = 0.25
f32 = jnp.float32
highest = lax.Precision.HIGHEST
BOTH = ("lat", "lon")


def iota(shape, dim):
    return lax.broadcasted_iota(jnp.int32, shape, dim)


def in_vmem(shape):
    return pltpu.VMEM(shape, f32)


def call(kernel, out_shapes, out=in_vmem, **kw):
    vm = pl.BlockSpec(memory_space=pltpu.VMEM)

    def run(*args):
        return pl.pallas_call(
            kernel,
            out_shape=[out(s) for s in out_shapes],
            in_specs=[vm] * len(args),
            out_specs=[vm] * len(out_shapes),
            **kw,
        )(*[pltpu.with_memory_space_constraint(a, pltpu.VMEM) for a in args])

    return run


RX = R + 16
LX = L + 2 * H
ROWS = slice(8, 8 + R)
COLS = slice(H, H + L)


def beyond(v, rows, cols):
    n, m = v.shape
    if rows:
        v = pltpu.roll(v, -rows % n, 0)
    if cols:
        v = pltpu.roll(v, -cols % m, 1)
    return v


def apply_faces(faces, v):
    return faces[4] * v - (
        faces[0] * beyond(v, 0, 1)
        + faces[1] * beyond(v, 0, -1)
        + faces[2] * beyond(v, 1, 0)
        + faces[3] * beyond(v, -1, 0)
    )


def tile_sums(fields):
    n = len(fields)
    pick = (iota((L, H), 0) // 64 == iota((L, H), 1) % 4).astype(f32)
    cols = jnp.dot(jnp.concatenate(fields, axis=0), pick, precision=highest, preferred_element_type=f32)
    keep = iota((R, H), 0) // 4 == (iota((R, H), 1) % 16) // 4
    return [
        jnp.sum(jnp.where(keep, cols[R * i : R * i + R], 0.0), axis=0, keepdims=True)
        for i in range(n)
    ]


def pack(rows, rho):
    block = iota((1, H), 1) // 16
    out = jnp.zeros((1, H), f32)
    for f, row in enumerate(rows):
        out = jnp.where(block == (f + rho) % 8, row, out)
    return out


def unpack(got, f):
    shape = (NDEV // 8, 8, H)
    keep = iota(shape, 2) // 16 == (iota(shape, 1) + f) % 8
    flat = jnp.sum(jnp.where(keep, got.reshape(shape), 0.0), axis=1)
    return pltpu.roll(flat, (H - 16 * f) % H, 1) if f else flat


def coarse_rows(c_ref, w):
    acc = jnp.zeros((R, H), f32)
    for r in range(NDEV // 8):
        acc = acc + c_ref[:, H * r : H * r + H] * w[r : r + 1, :]
    col = jnp.sum(acc, axis=1, keepdims=True)
    return jnp.sum(jnp.where(iota((R, H), 0) == iota((R, H), 1) % 16, col, 0.0), axis=0, keepdims=True)


G = (NDEV // 8, H)


def c_east(q):
    lane = iota(G, 1)
    near = pltpu.roll(q, H - 1, 1)
    far = pltpu.roll(q, H - 13, 1)
    swap = jnp.where(iota(G, 0) % 2 == 0, pltpu.roll(far, G[0] - 1, 0), pltpu.roll(far, 1, 0))
    far = jnp.where(lane // 16 == 7, swap, far)
    return jnp.where(lane % 4 == 3, far, near)


def c_west(q):
    lane = iota(G, 1)
    near = pltpu.roll(q, 1, 1)
    far = pltpu.roll(q, 13, 1)
    swap = jnp.where(iota(G, 0) % 2 == 0, pltpu.roll(far, G[0] - 1, 0), pltpu.roll(far, 1, 0))
    far = jnp.where(lane // 16 == 0, swap, far)
    return jnp.where(lane % 4 == 0, far, near)


def c_north(q):
    near = pltpu.roll(q, H - 4, 1)
    far = pltpu.roll(pltpu.roll(q, 12, 1), G[0] - 2, 0)
    return jnp.where((iota(G, 1) % 16) // 4 == 3, far, near)


def c_south(q):
    near = pltpu.roll(q, 4, 1)
    far = pltpu.roll(pltpu.roll(q, H - 12, 1), 2, 0)
    return jnp.where((iota(G, 1) % 16) // 4 == 0, far, near)


def coarse_operator(q, count, link_e, link_n):
    flux_e = link_e * (q - c_east(q))
    flux_n = link_n * (q - c_north(q))
    return EPS * count * q + (flux_e - c_west(flux_e)) + (flux_n - c_south(flux_n))


def total(v):
    return jnp.sum(jnp.sum(v, axis=0, keepdims=True), axis=1, keepdims=True)


def neighbour(la, lo, da, do):
    a = la + da
    there = jnp.logical_and(a >= 0, a < NLAT)
    a = jnp.clip(a, 0, NLAT - 1)
    return a * NLON + (lo + do + NLON) % NLON, there


def lane_column(row, f, o):
    lane = iota((R, H), 1)
    hit = (lane // 16 == (f + o) % 8) & (lane % 16 == iota((R, H), 0))
    return jnp.sum(jnp.where(hit, jnp.broadcast_to(row, (R, H)), 0.0), axis=1, keepdims=True)


def lane_value(row, f, o):
    hit = iota((1, H), 1) == 16 * ((f + o) % 8)
    return jnp.sum(jnp.where(hit, row, 0.0), axis=1, keepdims=True)


def column_lanes(v, c):
    return jnp.sum(
        jnp.where(iota((R, H), 0) == iota((R, H), 1) % 16, v[:, c : c + 1], 0.0), axis=0, keepdims=True
    )


def spread(got_ref, la, lo):
    row = iota((RX, H), 0)
    lane = iota((RX, H), 1)
    ty = jnp.where(row < 8, 3, jnp.where(row < 8 + R, (row - 8) // 4, 0))
    src = jnp.zeros((RX, H), f32)
    l2 = iota((H, LX), 0)
    c2 = iota((H, LX), 1)
    pick = jnp.zeros((H, LX), f32)
    for do in (-1, 0, 1):
        o = (lo + do + NLON) % NLON
        south, mine, north = [
            jnp.broadcast_to(got_ref[pl.ds(neighbour(la, lo, da, do)[0], 1), :], (RX, H)) for da in (-1, 0, 1)
        ]
        part = jnp.where(row < 8, south, jnp.where(row < 8 + R, mine, north))
        src = jnp.where((lane // 16 == o % 8) & ((lane % 16) // 4 == ty), part, src)
        if do == 0:
            to = (c2 >= H) & (c2 < H + L) & (l2 % 4 == (c2 - H) // 64)
        elif do < 0:
            to = (c2 < H) & (l2 % 4 == 3)
        else:
            to = (c2 >= H + L) & (l2 % 4 == 0)
        pick = jnp.where(to & (l2 // 16 == o % 8), 1.0, pick)
    return jnp.dot(src, pick, precision=highest, preferred_element_type=f32)


def prolong_row(q_row):
    keep = (iota((R, H), 1) < 16) & (iota((R, H), 1) // 4 == iota((R, H), 0) // 4)
    pick = (iota((H, L), 0) % 4 == iota((H, L), 1) // 64).astype(f32)
    return jnp.dot(
        jnp.where(keep, jnp.broadcast_to(q_row, (R, H)), 0.0), pick, precision=highest, preferred_element_type=f32
    )


CHUNKS = K // KB
NEAR = 0
FAR = 80
M_FORCE, M_WET1, M_WET2, M_DEPTH1, M_DEPTH2, M_X = range(6)
LAT_MISC = 160
LAT_ROWS = 168
LON_MISC = 2 * K
LON_LANES = 2 * H


def levels_kernel(thick, levels, mask, eta, rho, te, tn,
                  fe_out, fn_out, wet_out, x_out, depth_out, pe, pw, pn, ps,
                  t_s, lev_v, mask_v, eta_v, rho_v, te_v, tn_v, m8, a8, run, sem):
    small = [
        pltpu.make_async_copy(a, b, sem.at[3 * CHUNKS + i])
        for i, (a, b) in enumerate(((thick, t_s), (levels, lev_v), (mask, mask_v), (eta, eta_v)))
    ]
    for c in small:
        c.start()
    big = []
    for c in range(CHUNKS):
        part = pl.ds(c * KB, KB)
        big.append([
            pltpu.make_async_copy(a.at[part], b.at[part], sem.at[3 * c + i])
            for i, (a, b) in enumerate(((rho, rho_v), (te, te_v), (tn, tn_v)))
        ])
        for x in big[-1]:
            x.start()
    for c in small:
        c.wait()
    own = (lev_v[...] * mask_v[...]).astype(f32)
    wet_out[...] = own
    x_out[...] = mask_v[...].astype(f32) * eta_v[...]
    lane = iota((R, L), 1)
    row = iota((R, L), 0)
    for d, n in enumerate((1, 2)):
        m8[d] = jnp.where(lane < L - n, jnp.minimum(own, beyond(own, 0, n)), 0.0)
        m8[2 + d] = jnp.where(lane >= n, jnp.minimum(own, beyond(own, 0, -n)), 0.0)
        m8[4 + d] = jnp.where(row < R - n, jnp.minimum(own, beyond(own, n, 0)), 0.0)
        m8[6 + d] = jnp.where(row >= n, jnp.minimum(own, beyond(own, -n, 0)), 0.0)
    zero = jnp.zeros((8, H), f32)
    lane8 = iota((8, H), 1)
    for c in range(CHUNKS):
        for x in big[c]:
            x.wait()
        for a in range(2):
            for b in range(2):
                rs, ls = slice(8 * a, 8 * a + 8), slice(H * b, H * b + H)
                m = [m8[i, rs, ls] for i in range(8)]
                wet = wet_out[rs, ls]
                if c == 0:
                    p = g = d = fe = fn = zero
                    acc = [zero] * 8
                    prof = [zero, zero]
                else:
                    p, g = run[0, rs, ls], run[1, rs, ls]
                    d, fe, fn = depth_out[rs, ls], fe_out[rs, ls], fn_out[rs, ls]
                    acc = [a8[i, rs, ls] for i in range(8)]
                    lon_out = pe if b else pw
                    prof = [lon_out[rs, :H], lon_out[rs, H:]]
                for k in range(c * KB, c * KB + KB):
                    t = t_s[k]
                    p = p + t * rho_v[k, rs, ls]
                    g = g + t * p
                    ta = jnp.where(wet > float(k), t, 0.0)
                    d = d + ta
                    fe = fe + ta * te_v[k, rs, ls]
                    fn = fn + ta * tn_v[k, rs, ls]
                    acc = [jnp.where(mi > float(k), g, ai) for mi, ai in zip(m, acc)]
                    h, at = (2 * k) // H, (2 * k) % H
                    moved = pltpu.roll(g, (at + 2) % H if b else at, 1) if (at + 2 * b) % H else g
                    prof[h] = jnp.where((lane8 == at) | (lane8 == at + 1), moved, prof[h])
                    lat_out = pn if a else ps
                    near, far = (7, 6) if a else (0, 1)
                    lat_out[NEAR + k : NEAR + k + 1, ls] = g[near : near + 1]
                    lat_out[FAR + k : FAR + k + 1, ls] = g[far : far + 1]
                if c + 1 < CHUNKS:
                    run[0, rs, ls] = p
                    run[1, rs, ls] = g
                depth_out[rs, ls] = d
                fe_out[rs, ls] = fe
                fn_out[rs, ls] = fn
                for i in range(8):
                    a8[i, rs, ls] = acc[i]
                lon_out = pe if b else pw
                lon_out[rs, :H] = prof[0]
                lon_out[rs, H:] = prof[1]
    c1, c2 = 8.0 / 12.0, 1.0 / 12.0
    fe = fe_out[...] + c1 * (beyond(a8[0], 0, -1) - beyond(a8[2], 0, 1)) - c2 * (
        beyond(a8[1], 0, -2) - beyond(a8[3], 0, 2)
    )
    fn = fn_out[...] + c1 * (beyond(a8[4], -1, 0) - beyond(a8[6], 1, 0)) - c2 * (
        beyond(a8[5], -2, 0) - beyond(a8[7], 2, 0)
    )
    fe_out[...] = fe
    fn_out[...] = fn
    d = depth_out[...]
    x = x_out[...]
    lane_t = iota((R, H), 1)

    def lon_misc(out, force, wet, dep, xs, near, far):
        tile = out[:, H:]
        for i, (v, at) in enumerate(((force, near), (wet, near), (wet, far), (dep, near), (dep, far), (xs, near))):
            to = LON_MISC - H + i
            tile = jnp.where(lane_t == to, pltpu.roll(v, (to - at) % H, 1), tile)
        out[:, H:] = tile

    lon_misc(pe, fe[:, H:], own[:, H:], d[:, H:], x[:, H:], H - 1, H - 2)
    lon_misc(pw, fe[:, :H], own[:, :H], d[:, :H], x[:, :H], 0, 1)
    for out, near, far in ((pn, R - 1, R - 2), (ps, 0, 1)):
        for i, (v, at) in enumerate(((fn, near), (own, near), (own, far), (d, near), (d, far), (x, near))):
            out[LAT_MISC + i : LAT_MISC + i + 1] = v[at : at + 1]


def residual_kernel(fe_in, fn_in, wet, x0, depth, pe, pw, pn, ps, ge, gw, gn, gs,
                    res, scaled, dep_x, rows_n, rows_s, pay):
    own = wet[...]
    lane = iota((R, L), 1)
    row = iota((R, L), 0)

    def lon_misc(ref, i):
        return ref[:, LON_MISC + i : LON_MISC + i + 1]

    la, lo = lax.axis_index("lat"), lax.axis_index("lon")

    def lat_misc(ref, i):
        there = la < NLAT - 1 if ref is gn else la > 0
        return jnp.where(there, ref[LAT_MISC + i : LAT_MISC + i + 1], 0.0)

    def lon_pick(ref, m, col):
        at = 2 * m.astype(jnp.int32) - 2 + col
        return jnp.sum(jnp.where((lane == at) & (m > 0.0), ref[...], 0.0), axis=1, keepdims=True)

    level = iota((FAR, L), 0).astype(f32) + 1.0

    def lat_pick(ref, m, col):
        part = ref[FAR : 2 * FAR] if col else ref[NEAR : NEAR + FAR]
        return jnp.sum(jnp.where(level == m, part, 0.0), axis=0, keepdims=True)

    def cross(pick, got, sent, o1, o2, n1, n2, got_near, sent_near):
        gn_, sn_ = (0, 1) if got_near == 0 else (1, 0), (0, 1) if sent_near == 0 else (1, 0)
        first = (-8.0 * pick(got, jnp.minimum(o1, n1), gn_[0]) + pick(got, jnp.minimum(o1, n2), gn_[1])) / 12.0
        second = pick(got, jnp.minimum(o2, n1), gn_[0]) / 12.0
        theirs = (8.0 * pick(sent, jnp.minimum(n1, o1), sn_[0]) - pick(sent, jnp.minimum(n1, o2), sn_[1])) / 12.0
        return first, second, theirs

    fe = fe_in[...]
    fn = fn_in[...]
    a, b, far_e = cross(lon_pick, ge, pe, own[:, L - 1 :], own[:, L - 2 : L - 1],
                        lon_misc(ge, M_WET1), lon_misc(ge, M_WET2), 0, 1)
    fe = fe + jnp.where(lane == L - 1, a, 0.0) + jnp.where(lane == L - 2, b, 0.0)
    fe_e = lon_misc(ge, M_FORCE) + far_e
    a, b, far_w = cross(lon_pick, gw, pw, own[:, :1], own[:, 1:2],
                        lon_misc(gw, M_WET1), lon_misc(gw, M_WET2), 1, 0)
    fe = fe - jnp.where(lane == 0, a, 0.0) - jnp.where(lane == 1, b, 0.0)
    fe_w = lon_misc(gw, M_FORCE) - far_w
    a, b, far_n = cross(lat_pick, gn, pn, own[R - 1 :], own[R - 2 : R - 1],
                        lat_misc(gn, M_WET1), lat_misc(gn, M_WET2), 0, 0)
    fn = fn + jnp.where(row == R - 1, a, 0.0) + jnp.where(row == R - 2, b, 0.0)
    fn_n = lat_misc(gn, M_FORCE) + far_n
    a, b, far_s = cross(lat_pick, gs, ps, own[:1], own[1:2],
                        lat_misc(gs, M_WET1), lat_misc(gs, M_WET2), 0, 0)
    fn = fn - jnp.where(row == 0, a, 0.0) - jnp.where(row == 1, b, 0.0)
    fn_s = lat_misc(gs, M_FORCE) - far_s

    def shifts(v, e, w, n, s):
        return (
            jnp.where(lane == L - 1, e, beyond(v, 0, 1)),
            jnp.where(lane == 0, w, beyond(v, 0, -1)),
            jnp.where(row == R - 1, n, beyond(v, 1, 0)),
            jnp.where(row == 0, s, beyond(v, -1, 0)),
        )

    mask = (own > 0.0).astype(f32)
    d = depth[...]
    x = x0[...]
    face = [
        jnp.minimum(d, v)
        for v in shifts(d, lon_misc(ge, M_DEPTH1), lon_misc(gw, M_DEPTH1), lat_misc(gn, M_DEPTH1), lat_misc(gs, M_DEPTH1))
    ]
    diag = mask * (EPS + face[0] + face[1] + face[2] + face[3]) + (1.0 - mask)
    ax = diag * x
    for f, v in zip(face, shifts(x, lon_misc(ge, M_X), lon_misc(gw, M_X), lat_misc(gn, M_X), lat_misc(gs, M_X))):
        ax = ax - f * v
    f_e, f_w, _, _ = shifts(fe, fe_e, fe_w, fn_n, fn_s)
    _, _, f_n, f_s = shifts(fn, fe_e, fe_w, fn_n, fn_s)
    r = mask * 0.5 * (f_w - f_e + f_s - f_n) - ax
    s = r / diag
    res[...] = r
    scaled[...] = s
    rows_n[...] = s[8:]
    rows_s[...] = s[:8]
    dep_x[...] = jnp.zeros((RX, LX), f32)
    dep_x[ROWS, COLS] = d
    dep_x[7:8, COLS] = lat_misc(gs, M_DEPTH1)
    dep_x[6:7, COLS] = lat_misc(gs, M_DEPTH2)
    dep_x[8 + R : 9 + R, COLS] = lat_misc(gn, M_DEPTH1)
    dep_x[9 + R : 10 + R, COLS] = lat_misc(gn, M_DEPTH2)
    lane_t = iota((R, H), 1)
    dep_x[ROWS, :H] = jnp.where(
        lane_t == H - 1, lon_misc(gw, M_DEPTH1), jnp.where(lane_t == H - 2, lon_misc(gw, M_DEPTH2), 0.0)
    )
    dep_x[ROWS, H + L :] = jnp.where(
        lane_t == 0, lon_misc(ge, M_DEPTH1), jnp.where(lane_t == 1, lon_misc(ge, M_DEPTH2), 0.0)
    )
    rho = lo % 8
    (w,) = tile_sums([r * mask])
    pay[...] = jnp.broadcast_to(pack([w], rho), (NDEV, H))
    for do, c1, c2 in ((1, L - 1, L - 2), (-1, 0, 1)):
        at, _ = neighbour(la, lo, 0, do)
        pay[pl.ds(at, 1), :] = pack([w, column_lanes(s, c1), column_lanes(s, c2)], rho)
        for da, j in ((1, R - 1), (-1, 0)):
            at, there = neighbour(la, lo, da, do)
            at = jnp.where(there, at, la * NLON + lo)
            pay[pl.ds(at, 1), :] = pack(
                [w, jnp.broadcast_to(s[j : j + 1, c1 : c1 + 1], (1, H)), jnp.broadcast_to(d[j : j + 1, c1 : c1 + 1], (1, H))],
                rho,
            )


def first_kernel(got, coarse, res, scaled, dep_in, sn, ss, w_out, s_x, faces, pay):
    la, lo = lax.axis_index("lat"), lax.axis_index("lon")
    w = unpack(got[...], 0)
    w_out[...] = w
    q = coarse_rows(coarse, w)
    s = scaled[...]
    s_x[ROWS, COLS] = s
    s_x[:8, COLS] = jnp.where(la > 0, ss[...], 0.0)
    s_x[8 + R :, COLS] = jnp.where(la < NLAT - 1, sn[...], 0.0)
    lane = iota((R, H), 1)
    dep = dep_in[...]
    dep_x = faces.at[4]
    dep_x[...] = dep
    for do, cols, l1, l2 in ((1, slice(H + L, LX), 0, 1), (-1, slice(0, H), H - 1, H - 2)):
        at, _ = neighbour(la, lo, 0, do)
        o = (lo + do + NLON) % NLON
        msg = got[pl.ds(at, 1), :]
        s_x[ROWS, cols] = jnp.where(lane == l1, lane_column(msg, 1, o), jnp.where(lane == l2, lane_column(msg, 2, o), 0.0))
        for da, rows, j in ((1, slice(8 + R, RX), 0), (-1, slice(0, 8), 7)):
            at, there = neighbour(la, lo, da, do)
            msg = got[pl.ds(at, 1), :]
            here = (iota((8, H), 0) == j) & (iota((8, H), 1) == l1) & there
            s_x[rows, cols] = jnp.where(here, lane_value(msg, 1, o), 0.0)
            dep_x[rows, cols] = jnp.where(here, lane_value(msg, 2, o), 0.0)
    d = dep_x[...]
    mask = (d > 0.0).astype(f32)
    face = [jnp.minimum(d, beyond(d, a, b)) for a, b in ((0, 1), (0, -1), (1, 0), (-1, 0))]
    for i in range(4):
        faces[i] = face[i]
    diag = mask * (EPS + face[0] + face[1] + face[2] + face[3]) + (1.0 - mask)
    faces[4] = diag
    faces[5] = mask
    own = (ROWS, COLS)
    a_s = apply_faces(face + [diag], s_x[...])[own]
    sums = tile_sums([
        a_s * mask[own],
        mask[own],
        jnp.where(iota((R, L), 1) % 64 == 63, face[0][own], 0.0),
        jnp.where(iota((R, L), 0) % 4 == 3, face[2][own], 0.0),
        s * a_s,
        res[...] * s,
    ])
    pay[...] = jnp.broadcast_to(pack([q] + sums, lo % 8), (NDEV, H))


def step_kernel(got, coarse, w_in, res, s_x, faces, x0,
                r_out, s_out, as_out, x_out, d_out, ad_out, w_out, u_out, net_out, num_out, pay):
    la, lo = lax.axis_index("lat"), lax.axis_index("lon")
    own = (ROWS, COLS)
    g = got[...]
    q, a, count, link_e, link_n, cc, ee = [unpack(g, f) for f in range(7)]
    w = w_in[...]
    tq = coarse_operator(q, count, link_e, link_n)
    u = a + tq
    d_a_d = total(cc + q * (2.0 * a + tq))
    rz = total(ee + w * q)
    alpha = rz / d_a_d
    w = w - alpha * u
    w_out[...] = w
    u_out[...] = u
    net_out[0] = count
    net_out[1] = link_e
    net_out[2] = link_n
    num_out[0:1] = jnp.broadcast_to(rz, (1, H))
    num_out[1:2] = jnp.broadcast_to(d_a_d, (1, H))
    num_out[2:] = jnp.zeros((6, H), f32)
    q = coarse_rows(coarse, w)
    face = [faces[i] for i in range(6)]
    mask = face[5]
    s = s_x[...]
    d = s + mask * spread(got, la, lo)
    ad = apply_faces(face, d)
    s = s - alpha * (ad / face[4])
    a_s = apply_faces(face, s)[own]
    ad = ad[own]
    s = s[own]
    r = res[...] - alpha * ad
    r_out[...] = r
    s_out[...] = s
    as_out[...] = a_s
    x_out[...] = x0[...] + alpha * d[own]
    d_out[...] = d[own]
    ad_out[...] = ad
    sums = tile_sums([a_s * mask[own], s * a_s, r * s, s * ad])
    pay[...] = jnp.broadcast_to(pack([q] + sums, lo % 8), (NDEV, H))


def last_kernel(got, w_in, u_in, net, num, coarse, res, scaled, a_s, ad, d_in, x_in, faces, surface, precond):
    la, lo = lax.axis_index("lat"), lax.axis_index("lon")
    own = (ROWS, COLS)
    g = got[...]
    q, a, cc, ee, hh = [unpack(g, f) for f in range(5)]
    w = w_in[...]
    u0 = u_in[...]
    rz0 = num[0:1, :1]
    dad0 = num[1:2, :1]
    tq = coarse_operator(q, net[0], net[1], net[2])
    zaz = total(cc + q * (2.0 * a + tq))
    rz = total(ee + w * q)
    zad = total(hh + q * u0)
    beta = rz / rz0
    alpha = rz / (zaz + 2.0 * beta * zad + beta * beta * dad0)
    q2 = prolong_row(coarse_rows(coarse, w - alpha * (a + tq + beta * u0)))
    face = [faces[i] for i in range(6)]
    mask = face[5]
    pq = mask * spread(got, la, lo)
    d = scaled[...] + pq[own] + beta * d_in[...]
    ad1 = a_s[...] + apply_faces(face, pq)[own] + beta * ad[...]
    surface[...] = x_in[...] + alpha * d
    precond[...] = (res[...] - alpha * ad1) / face[4][own] + q2 * mask[own]


def to_east(v):
    return lax.ppermute(v, "lon", [(i, (i + 1) % NLON) for i in range(NLON)])


def to_west(v):
    return lax.ppermute(v, "lon", [((i + 1) % NLON, i) for i in range(NLON)])


def to_north(v):
    return lax.ppermute(v, "lat", [(i, (i + 1) % NLAT) for i in range(NLAT)])


def to_south(v):
    return lax.ppermute(v, "lat", [((i + 1) % NLAT, i) for i in range(NLAT)])


def gather(pay):
    return lax.all_to_all(pay, BOTH, 0, 0, tiled=True)


def body(density, tend_east, tend_north, thickness, levels, ocean_mask, eta_prev, coarse):
    plane, wide = (R, L), (RX, LX)
    lon_msg, lat_msg = (R, LON_LANES), (LAT_ROWS, L)
    vm = pl.BlockSpec(memory_space=pltpu.VMEM)
    fe, fn, wet, x0, depth, pe, pw, pn, ps = pl.pallas_call(
        levels_kernel,
        in_specs=[pl.BlockSpec(memory_space=pl.ANY)] * 7,
        out_specs=[vm] * 9,
        out_shape=[in_vmem(s) for s in [plane] * 5 + [lon_msg] * 2 + [lat_msg] * 2],
        scratch_shapes=[
            pltpu.SMEM((K,), f32),
            pltpu.VMEM(plane, jnp.int32),
            pltpu.VMEM(plane, jnp.int32),
            pltpu.VMEM(plane, f32),
            pltpu.VMEM((K, R, L), f32),
            pltpu.VMEM((K, R, L), f32),
            pltpu.VMEM((K, R, L), f32),
            pltpu.VMEM((8, R, L), f32),
            pltpu.VMEM((8, R, L), f32),
            pltpu.VMEM((2, R, L), f32),
            pltpu.SemaphoreType.DMA((3 * CHUNKS + 4,)),
        ],
        name="levels",
    )(thickness, levels, ocean_mask, eta_prev, density, tend_east, tend_north)
    gn, gs = to_south(ps), to_north(pn)
    ge, gw = to_west(pw), to_east(pe)
    r0, s0, dep_x, rows_n, rows_s, pay = call(
        residual_kernel, [plane, plane, wide, (8, L), (8, L), (NDEV, H)]
    )(fe, fn, wet, x0, depth, pe, pw, pn, ps, ge, gw, gn, gs)
    sn, ss = to_south(rows_s), to_north(rows_n)
    got = gather(pay)
    w0, s_x, faces, pay = call(first_kernel, [G, wide, (6,) + wide, (NDEV, H)])(got, coarse, r0, s0, dep_x, sn, ss)
    got = gather(pay)
    r1, s1, as1, x1, d0, ad0, w1, u0, net, num, pay = call(
        step_kernel, [plane] * 6 + [G, G, (3,) + G, (8, H), (NDEV, H)]
    )(got, coarse, w0, r0, s_x, faces, x0)
    got = gather(pay)
    return tuple(
        call(last_kernel, [plane, plane], out=lambda s: jax.ShapeDtypeStruct(s, f32))(
            got, w1, u0, net, num, coarse, r1, s1, as1, ad0, d0, x1, faces
        )
    )


def solution(mesh):
    return jax.shard_map(
        body,
        mesh=mesh,
        in_specs=(
            P(None, "lat", "lon"),
            P(None, "lat", "lon"),
            P(None, "lat", "lon"),
            P(),
            P("lat", "lon"),
            P("lat", "lon"),
            P("lat", "lon"),
            P(("lat", "lon"), None),
        ),
        out_specs=(P("lat", "lon"), P("lat", "lon")),
        check_vma=False,
    )
```

time: 527 us -> 83.3 us (0.16)
  blocking collectives: 458 us -> 36.9 us
  other arithmetic: 9.79 us -> 0 us
  Pallas kernels: 0 us -> 7.08 us
  local copies, waits for them, and re-layouts: 5.91 us -> 0.01 us
    psum x3 -> x0, blocking collectives: 231 us -> none  [global_sum(): return lax.psum(partial_value, ('lat', 'lon'))]
    unnamed x3 -> x0, blocking collectives: 227 us -> none
    all_to_all x0 -> x2, blocking collectives: none -> 36.9 us  [gather(): return lax.all_to_all(pay, BOTH, 0, 0, tiled=True)]
    ppermute x16 -> x6, starting transfers between devices: 28.2 us -> 10.2 us  [the longest x1 3.78 us: to_west(): return lax.ppermute(v, 'lon', [((i + 1) % NLON, i) for i in range(NLON)])]
    all_to_all x0 -> x1, starting transfers between devices: none -> 16.2 us  [gather(): return lax.all_to_all(pay, BOTH, 0, 0, tiled=True)]
    ppermute x16 -> x6, waiting for transfers between devices: 14.2 us -> 4.35 us  [the longest x2 1.7 us: to_north(): return lax.ppermute(v, 'lat', [(i, (i + 1) % NLAT) for i in range(NLAT)])]
    all_to_all x0 -> x1, waiting for transfers between devices: none -> 7.67 us  [gather(): return lax.all_to_all(pay, BOTH, 0, 0, tiled=True)]
    pallas_call x0 -> x5, Pallas kernels: none -> 7.08 us  [the longest x4 4.09 us: run(): pl.pallas_call(kernel, out_shape=[out(s) for s in out_shapes], in_specs=[...]
  transfers between devices with their start and end apart: 16 -> 7, of which waited for: 12 -> 4; matrix products, arithmetic and copies ran while one was open for 0% -> 0% of each run, Pallas kernels for 0% -> 0%
where the time goes in v1:
time: 83.3 us; the launch traced here: 83.1 us
  blocking collectives  36.9 us (44%)
  starting transfers between devices  26.4 us (32%)
  waiting for transfers between devices  12 us (14%)
  Pallas kernels  7.08 us (8%)
    all_to_all x2, blocking collectives, gather(): return lax.all_to_all(pay, BOTH, 0, 0, tiled=True)  36.9 us
    all_to_all x1, starting transfers between devices, gather(): return lax.all_to_all(pay, BOTH, 0, 0, tiled=True)  16.2 us
    all_to_all x1, waiting for transfers between devices, gather(): return lax.all_to_all(pay, BOTH, 0, 0, tiled=True)  7.67 us
    pallas_call x4, Pallas kernels, run(): pl.pallas_call(kernel, out_shape=[out(s) for s in out_shapes], in_specs=[...  4.09 us
    ppermute x1, starting transfers between devices, to_west(): return lax.ppermute(v, 'lon', [((i + 1) % NLON, i) for i in range(NLON)])  3.78 us
    ppermute x2, starting transfers between devices, to_north(): return lax.ppermute(v, 'lat', [(i, (i + 1) % NLAT) for i in range(NLAT)])  3.03 us
    pallas_call x1, Pallas kernels, body(): pl.pallas_call(levels_kernel, in_specs=[pl.BlockSpec(memory_space=pl.ANY)...  2.99 us
    ppermute x2, starting transfers between devices, to_south(): return lax.ppermute(v, 'lat', [((i + 1) % NLAT, i) for i in range(NLAT)])  2.37 us
  transfers between devices with their start and end apart: 7, of which 4 were waited for; matrix products, arithmetic and copies ran while one was open for 0% of the time, Pallas kernels for 0%

profile of v1, /device:TPU:1, one launch (start us, length us, event | category | flops | bytes accessed | tf_op | source)
XLA Modules:
  0.0 83.1 jit_solution(17546609614430606690)
XLA Ops:
  0.6 3.0 %levels.2 = (f32[16,256]{1,0:T(8,128)S(1)}, f32[16,256]{1,0:T(8,128)S(1)}, f32[16,256]{1,0:T(8,128)S(1)}, f32[16,256]{1,0:T(8,128)S(1)}, f32[16,256]{1,0:T(8,128...) custom-call(f32[75]{0:T(128)} %thick.1, ...), custom_call_target="tpu_custom_call" | custom-call | tf_op jit(solution)/shard_map/levels/pallas_call | solution.py:559
  3.6 0.0 copy-start
  3.6 3.0 %collective-permute-start.3 = (f32[168,256]{1,0:T(8,128)S(1)}, f32[168,256]{1,0:T(8,128)S(1)}, u32[]{:S(2)}, u32[]{:S(2)}) collective-permute-start(f32[168,256]{1,0:T(8,128)S(1)} %get-tuple-element.39.pn), channel_id=1, source_target_pairs={{0,16},{16,32},{32,48},{48,64},{64,80},{80,96},{96,112},{112,128},... | collective-permute-start | bytes 516104 | tf_op jit(solution)/shard_map/ppermute | solution.py:544
  6.7 0.2 collective-permute-start.2
  6.9 1.0 %collective-permute-start.1 = (f32[16,256]{1,0:T(8,128)S(1)}, f32[16,256]{1,0:T(8,128)S(1)}, u32[]{:S(2)}, u32[]{:S(2)}) collective-permute-start(f32[16,256]{1,0:T(8,128)S(1)} %get-tuple-element.37.pe), channel_id=1, source_target_pairs={{0,1},{1,2},{2,3},{3,4},{4,5},{5,6},{6,7},{7,8},{8,9},{9,10},{10,1... | collective-permute-start | bytes 49160 | tf_op jit(solution)/shard_map/ppermute | solution.py:536
  7.9 3.8 %collective-permute-start = (f32[16,256]{1,0:T(8,128)S(1)}, f32[16,256]{1,0:T(8,128)S(1)}, u32[]{:S(2)}, u32[]{:S(2)}) collective-permute-start(f32[16,256]{1,0:T(8,128)S(1)} %get-tuple-element.38.pw), channel_id=1, source_target_pairs={{1,0},{2,1},{3,2},{4,3},{5,4},{6,5},{7,6},{8,7},{9,8},{10,9},{11,1... | collective-permute-start | bytes 49160 | tf_op jit(solution)/shard_map/ppermute | solution.py:540
  11.7 1.1 %collective-permute-done.1.gw = f32[16,256]{1,0:T(8,128)S(1)} collective-permute-done((f32[16,256]{1,0:T(8,128)S(1)}, f32[16,256]{1,0:T(8,128)S(1)}, u32[]{:S(2)}, u32[]{:S(2)}) %collective-permute-start.1) | collective-permute-done | bytes 16416 | tf_op jit(solution)/shard_map/ppermute | solution.py:536
  12.8 0.0 collective-permute-done.ge
  12.8 0.0 collective-permute-done.3.gs
  12.8 0.0 collective-permute-done.2.gn
  12.8 1.3 %shard_map.95 = (f32[16,256]{1,0:T(8,128)S(1)}, f32[16,256]{1,0:T(8,128)S(1)}, f32[32,512]{1,0:T(8,128)S(1)}, f32[8,256]{1,0:T(8,128)S(1)}, f32[8,256]{1,0:T(8,128)S(1)}, /*index=5*/f32[256,128]{1,0:T(8,128)}) custom-call(f32[16,256]{1,0:T(8,128)S(1)} %get-tuple-element.32.fe_in, f32[16,256]{1,0:T(8,128)S(1)} %get-tuple-element.33.fn_in, ...), custom_call_target="tpu_custom_call" | custom-call | tf_op jit(solution)/shard_map/pallas_call | solution.py:34
  14.1 16.2 %all-to-all-start = ((f32[256,1,128]{2,1,0:T(1,128)}), f32[256,1,128]{2,1,0:T(1,128)S(1)}, u32[]{:S(2)}, u32[]{:S(2)}) async-start(f32[256,1,128]{2,1,0:T(1,128)} %bitcast.1), calls=%async_computation | async-start | bytes 262144 | tf_op jit(solution)/shard_map/all_to_all | solution.py:552
  30.4 2.2 %collective-permute-start.4 = (f32[8,256]{1,0:T(8,128)S(1)}, f32[8,256]{1,0:T(8,128)S(1)}, u32[]{:S(2)}, u32[]{:S(2)}) collective-permute-start(f32[8,256]{1,0:T(8,128)S(1)} %get-tuple-element.45), channel_id=1, source_target_pairs={{16,0},{32,16},{48,32},{64,48},{80,64},{96,80},{112,96},{128,112},... | collective-permute-start | bytes 24584 | tf_op jit(solution)/shard_map/ppermute | solution.py:548
  32.5 0.0 collective-permute-start.5
  32.5 1.5 %collective-permute-done.4.sn = f32[8,256]{1,0:T(8,128)S(1)} collective-permute-done((f32[8,256]{1,0:T(8,128)S(1)}, f32[8,256]{1,0:T(8,128)S(1)}, u32[]{:S(2)}, u32[]{:S(2)}) %collective-permute-start.4) | collective-permute-done | bytes 8224 | tf_op jit(solution)/shard_map/ppermute | solution.py:548
  34.0 1.7 %collective-permute-done.5.ss = f32[8,256]{1,0:T(8,128)S(1)} collective-permute-done((f32[8,256]{1,0:T(8,128)S(1)}, f32[8,256]{1,0:T(8,128)S(1)}, u32[]{:S(2)}, u32[]{:S(2)}) %collective-permute-start.5) | collective-permute-done | bytes 8224 | tf_op jit(solution)/shard_map/ppermute | solution.py:544
  35.7 7.7 %all-to-all-done = f32[256,1,128]{2,1,0:T(1,128)S(1)} async-done(((f32[256,1,128]{2,1,0:T(1,128)}), f32[256,1,128]{2,1,0:T(1,128)S(1)}, u32[]{:S(2)}, u32[]{:S(2)}) %all-to-all-start) | async-done | bytes 131104 | tf_op jit(solution)/shard_map/all_to_all | solution.py:552
  43.4 0.0 copy-done
  43.4 0.4 shard_map.96
  43.8 18.4 %all_to_all.33 = f32[256,1,128]{2,1,0:T(1,128)S(1)} all-to-all(f32[256,1,128]{2,1,0:T(1,128)S(1)} %bitcast.16), channel_id=1, replica_groups=mesh['lat'=16,'lon'=16] {'lat','lon'}, dimensions={0} | all-to-all | bytes 262144 | tf_op jit(solution)/shard_map/all_to_all | solution.py:552
  62.3 0.9 %shard_map.97 = (f32[16,256]{1,0:T(8,128)S(1)}, f32[16,256]{1,0:T(8,128)S(1)}, f32[16,256]{1,0:T(8,128)S(1)}, f32[16,256]{1,0:T(8,128)S(1)}, f32[16,256]{1,0:T(8...) custom-call(f32[256,128]{1,0:T(8,128)S(1)} %bitcast.12, ...), custom_call_target="tpu_custom_call" | custom-call | tf_op jit(solution)/shard_map/pallas_call | solution.py:34
  63.1 18.4 %all_to_all.34 = f32[256,1,128]{2,1,0:T(1,128)S(1)} all-to-all(f32[256,1,128]{2,1,0:T(1,128)S(1)} %bitcast.15), channel_id=1, replica_groups=mesh['lat'=16,'lon'=16] {'lat','lon'}, dimensions={0} | all-to-all | bytes 262144 | tf_op jit(solution)/shard_map/all_to_all | solution.py:552
  81.6 1.5 %shard_map.98 = (f32[16,256]{1,0:T(8,128)}, f32[16,256]{1,0:T(8,128)}) custom-call(f32[256,128]{1,0:T(8,128)S(1)} %bitcast.14, f32[32,128]{1,0:T(8,128)S(1)} %get-tuple-element.52.w_in, f32[32,128]{1,0:T(8,128)S(1)} %get-tuple-element.53.u_in, f32[3,32,128]{2,1,0:T(8,128)S(1)} %get-tuple-element.54.net, f32[8,128]{1,0:T(8,128)S(1)} %get-tuple-element.55.num, ...), custom_call_target="tpu_custom_call" | custom-call | tf_op jit(solution)/shard_map/pallas_call | solution.py:34
Async XLA Ops:
  3.6 39.8 %copy-start = (f32[16,4096]{1,0:T(8,128)S(1)}, f32[16,4096]{1,0:T(8,128)}, u32[]{:S(2)}) copy-start(f32[16,4096]{1,0:T(8,128)} %coarse.5) | copy-start | bytes 786436
  3.6 9.2 %collective-permute-start.3 = (f32[168,256]{1,0:T(8,128)S(1)}, f32[168,256]{1,0:T(8,128)S(1)}, u32[]{:S(2)}, u32[]{:S(2)}) collective-permute-start(f32[168,256]{1,0:T(8,128)S(1)} %get-tuple-element.39.pn), channel_id=1, source_target_pairs={{0,16},{16,32},{32,48},{48,64},{64,80},{80,96},{96,112},{112,128},... | collective-permute-start | bytes 516104 | tf_op jit(solution)/shard_map/ppermute | solution.py:544
  6.7 6.1 %collective-permute-start.2 = (f32[168,256]{1,0:T(8,128)S(1)}, f32[168,256]{1,0:T(8,128)S(1)}, u32[]{:S(2)}, u32[]{:S(2)}) collective-permute-start(f32[168,256]{1,0:T(8,128)S(1)} %get-tuple-element.40.ps), channel_id=1, source_target_pairs={{16,0},{32,16},{48,32},{64,48},{80,64},{96,80},{112,96},{128,112},... | collective-permute-start | bytes 516104 | tf_op jit(solution)/shard_map/ppermute | solution.py:548
  6.9 5.9 %collective-permute-start.1 = (f32[16,256]{1,0:T(8,128)S(1)}, f32[16,256]{1,0:T(8,128)S(1)}, u32[]{:S(2)}, u32[]{:S(2)}) collective-permute-start(f32[16,256]{1,0:T(8,128)S(1)} %get-tuple-element.37.pe), channel_id=1, source_target_pairs={{0,1},{1,2},{2,3},{3,4},{4,5},{5,6},{6,7},{7,8},{8,9},{9,10},{10,1... | collective-permute-start | bytes 49160 | tf_op jit(solution)/shard_map/ppermute | solution.py:536
  7.9 4.9 %collective-permute-start = (f32[16,256]{1,0:T(8,128)S(1)}, f32[16,256]{1,0:T(8,128)S(1)}, u32[]{:S(2)}, u32[]{:S(2)}) collective-permute-start(f32[16,256]{1,0:T(8,128)S(1)} %get-tuple-element.38.pw), channel_id=1, source_target_pairs={{1,0},{2,1},{3,2},{4,3},{5,4},{6,5},{7,6},{8,7},{9,8},{10,9},{11,1... | collective-permute-start | bytes 49160 | tf_op jit(solution)/shard_map/ppermute | solution.py:540
  14.1 29.3 %all-to-all-start = ((f32[256,1,128]{2,1,0:T(1,128)}), f32[256,1,128]{2,1,0:T(1,128)S(1)}, u32[]{:S(2)}, u32[]{:S(2)}) async-start(f32[256,1,128]{2,1,0:T(1,128)} %bitcast.1), calls=%async_computation | async-start | bytes 262144 | tf_op jit(solution)/shard_map/all_to_all | solution.py:552
  30.4 3.7 %collective-permute-start.4 = (f32[8,256]{1,0:T(8,128)S(1)}, f32[8,256]{1,0:T(8,128)S(1)}, u32[]{:S(2)}, u32[]{:S(2)}) collective-permute-start(f32[8,256]{1,0:T(8,128)S(1)} %get-tuple-element.45), channel_id=1, source_target_pairs={{16,0},{32,16},{48,32},{64,48},{80,64},{96,80},{112,96},{128,112},... | collective-permute-start | bytes 24584 | tf_op jit(solution)/shard_map/ppermute | solution.py:548
  32.5 3.2 %collective-permute-start.5 = (f32[8,256]{1,0:T(8,128)S(1)}, f32[8,256]{1,0:T(8,128)S(1)}, u32[]{:S(2)}, u32[]{:S(2)}) collective-permute-start(f32[8,256]{1,0:T(8,128)S(1)} %get-tuple-element.46), channel_id=1, source_target_pairs={{0,16},{16,32},{32,48},{48,64},{64,80},{80,96},{96,112},{112,128},... | collective-permute-start | bytes 24584 | tf_op jit(solution)/shard_map/ppermute | solution.py:544

commit v2 on v1

--- a/solution.py
+++ b/solution.py
@@ -6,7 +6,6 @@
 from jax.sharding import PartitionSpec as P
 
 K = 75
-KB = 15
 R = 16
 L = 256
 H = 128
@@ -200,7 +199,8 @@
     )
 
 
-CHUNKS = K // KB
+BOUNDS = (0, 20, 45, K)
+CHUNKS = len(BOUNDS) - 1
 NEAR = 0
 FAR = 80
 M_FORCE, M_WET1, M_WET2, M_DEPTH1, M_DEPTH2, M_X = range(6)
@@ -208,11 +208,23 @@
 LAT_ROWS = 168
 LON_MISC = 2 * K
 LON_LANES = 2 * H
+C1, C2 = 8.0 / 12.0, 1.0 / 12.0
+
+
+def lon_pick(prof, m, col, stride=2):
+    at = stride * m.astype(jnp.int32) - stride + col
+    lane = iota(prof.shape, 1)
+    return jnp.sum(jnp.where((lane == at) & (m > 0.0), prof, 0.0), axis=1, keepdims=True)
+
+
+def lat_pick(prof, m):
+    level = iota((FAR, L), 0).astype(f32) + 1.0
+    return jnp.sum(jnp.where(level == m, prof, 0.0), axis=0, keepdims=True)
 
 
 def levels_kernel(thick, levels, mask, eta, rho, te, tn,
-                  fe_out, fn_out, wet_out, x_out, depth_out, pe, pw, pn, ps,
-                  t_s, lev_v, mask_v, eta_v, rho_v, te_v, tn_v, m8, a8, run, sem):
+                  prefix, fe_out, fn_out, wet_out, x_out, depth_out, pe, pw, pn, ps, lat_a, lat_b, lon_a, lon_b,
+                  t_s, lev_v, mask_v, eta_v, rho_v, te_v, tn_v, run, lon3, lat3, sem):
     small = [
         pltpu.make_async_copy(a, b, sem.at[3 * CHUNKS + i])
         for i, (a, b) in enumerate(((thick, t_s), (levels, lev_v), (mask, mask_v), (eta, eta_v)))
@@ -220,19 +232,104 @@
     for c in small:
         c.start()
     big = []
-    for c in range(CHUNKS):
-        part = pl.ds(c * KB, KB)
-        big.append([
-            pltpu.make_async_copy(a.at[part], b.at[part], sem.at[3 * c + i])
-            for i, (a, b) in enumerate(((rho, rho_v), (te, te_v), (tn, tn_v)))
-        ])
-        for x in big[-1]:
-            x.start()
+    for i, (a, b) in enumerate(((rho, rho_v), (te, te_v), (tn, tn_v))):
+        big.append([])
+        for c in range(CHUNKS):
+            part = pl.ds(BOUNDS[c], BOUNDS[c + 1] - BOUNDS[c])
+            big[-1].append(pltpu.make_async_copy(a.at[part], b.at[part], sem.at[CHUNKS * i + c]))
+            big[-1][-1].start()
     for c in small:
         c.wait()
     own = (lev_v[...] * mask_v[...]).astype(f32)
     wet_out[...] = own
     x_out[...] = mask_v[...].astype(f32) * eta_v[...]
+    zero = jnp.zeros((8, H), f32)
+    lane8 = iota((8, H), 1)
+    blocks = [(a, b, slice(8 * a, 8 * a + 8), slice(H * b, H * b + H)) for a in range(2) for b in range(2)]
+    for a, b, rs, ls in blocks:
+        d = zero
+        wet = wet_out[rs, ls]
+        for k in range(K):
+            d = d + jnp.where(wet > float(k), t_s[k], 0.0)
+        depth_out[rs, ls] = d
+    for c in range(CHUNKS):
+        big[0][c].wait()
+        for a, b, rs, ls in blocks:
+            lon_out = pe if b else pw
+            if c == 0:
+                p = g = third = zero
+                prof = [zero, zero]
+            else:
+                p, g = run[0, rs, ls], run[1, rs, ls]
+                prof = [lon_out[rs, :H], lon_out[rs, H:]]
+                third = lon3[b, rs]
+            for k in range(BOUNDS[c], BOUNDS[c + 1]):
+                t = t_s[k]
+                p = p + t * rho_v[k, rs, ls]
+                g = g + t * p
+                prefix[k, rs, ls] = g
+                h, at = (2 * k) // H, (2 * k) % H
+                moved = pltpu.roll(g, (at + 2) % H if b else at, 1) if (at + 2 * b) % H else g
+                prof[h] = jnp.where((lane8 == at) | (lane8 == at + 1), moved, prof[h])
+                shift = (k - (H - 3 if b else 2)) % H
+                third = jnp.where(lane8 == k, pltpu.roll(g, shift, 1) if shift else g, third)
+                lat_out = pn if a else ps
+                near, far, past = (7, 6, 5) if a else (0, 1, 2)
+                lat_out[NEAR + k : NEAR + k + 1, ls] = g[near : near + 1]
+                lat_out[FAR + k : FAR + k + 1, ls] = g[far : far + 1]
+                lat3[a, k : k + 1, ls] = g[past : past + 1]
+            if c + 1 < CHUNKS:
+                run[0, rs, ls] = p
+                run[1, rs, ls] = g
+            lon_out[rs, :H] = prof[0]
+            lon_out[rs, H:] = prof[1]
+            lon3[b, rs] = third
+    for copies, tend, out in ((big[1], te_v, fe_out), (big[2], tn_v, fn_out)):
+        for c in range(CHUNKS):
+            copies[c].wait()
+            for a, b, rs, ls in blocks:
+                f = out[rs, ls] if c else zero
+                wet = wet_out[rs, ls]
+                for k in range(BOUNDS[c], BOUNDS[c + 1]):
+                    f = f + jnp.where(wet > float(k), t_s[k], 0.0) * tend[k, rs, ls]
+                out[rs, ls] = f
+    fe, fn, d, x = fe_out[...], fn_out[...], depth_out[...], x_out[...]
+    lane_t = iota((R, H), 1)
+
+    def column(v, c):
+        return v[:, c : c + 1]
+
+    def line(v, r):
+        return v[r : r + 1]
+
+    for out, b, far_at, sign, c0, c1, c2 in ((pe, 1, 0, 1.0, L - 1, L - 2, L - 3), (pw, 0, 1, -1.0, 0, 1, 2)):
+        o = column(own, c0)
+        near = lon_pick(out[...], jnp.minimum(o, column(own, c1)), far_at)
+        past = lon_pick(lon3[b], jnp.minimum(o, column(own, c2)), 0, 1)
+        force = column(fe, c0) + sign * (C1 * near - C2 * past)
+        tile = out[:, H:]
+        for i, v in enumerate((force, o, column(own, c1), column(d, c0), column(d, c1), column(x, c0))):
+            tile = jnp.where(lane_t == LON_MISC - H + i, v, tile)
+        out[:, H:] = tile
+    for out, a, sign, r0, r1, r2 in ((pn, 1, 1.0, R - 1, R - 2, R - 3), (ps, 0, -1.0, 0, 1, 2)):
+        o = line(own, r0)
+        near = lat_pick(out[FAR : 2 * FAR], jnp.minimum(o, line(own, r1)))
+        past = lat_pick(lat3[a], jnp.minimum(o, line(own, r2)))
+        force = line(fn, r0) + sign * (C1 * near - C2 * past)
+        for i, v in enumerate((force, o, line(own, r1), line(d, r0), line(d, r1), line(x, r0))):
+            out[LAT_MISC + i : LAT_MISC + i + 1] = v
+    even = lax.axis_index("lat") % 2 == 0
+    n, s = pn[...], ps[...]
+    lat_a[...] = jnp.where(even, n, s)
+    lat_b[...] = jnp.where(even, s, n)
+    even = lax.axis_index("lon") % 2 == 0
+    e, w = pe[...], pw[...]
+    lon_a[...] = jnp.where(even, e, w)
+    lon_b[...] = jnp.where(even, w, e)
+
+
+def inner_kernel(prefix, wet, te, tn, fe_out, fn_out, m8, a8):
+    own = wet[...]
     lane = iota((R, L), 1)
     row = iota((R, L), 0)
     for d, n in enumerate((1, 2)):
@@ -240,104 +337,50 @@
         m8[2 + d] = jnp.where(lane >= n, jnp.minimum(own, beyond(own, 0, -n)), 0.0)
         m8[4 + d] = jnp.where(row < R - n, jnp.minimum(own, beyond(own, n, 0)), 0.0)
         m8[6 + d] = jnp.where(row >= n, jnp.minimum(own, beyond(own, -n, 0)), 0.0)
-    zero = jnp.zeros((8, H), f32)
-    lane8 = iota((8, H), 1)
-    for c in range(CHUNKS):
-        for x in big[c]:
-            x.wait()
-        for a in range(2):
-            for b in range(2):
-                rs, ls = slice(8 * a, 8 * a + 8), slice(H * b, H * b + H)
-                m = [m8[i, rs, ls] for i in range(8)]
-                wet = wet_out[rs, ls]
-                if c == 0:
-                    p = g = d = fe = fn = zero
-                    acc = [zero] * 8
-                    prof = [zero, zero]
-                else:
-                    p, g = run[0, rs, ls], run[1, rs, ls]
-                    d, fe, fn = depth_out[rs, ls], fe_out[rs, ls], fn_out[rs, ls]
-                    acc = [a8[i, rs, ls] for i in range(8)]
-                    lon_out = pe if b else pw
-                    prof = [lon_out[rs, :H], lon_out[rs, H:]]
-                for k in range(c * KB, c * KB + KB):
-                    t = t_s[k]
-                    p = p + t * rho_v[k, rs, ls]
-                    g = g + t * p
-                    ta = jnp.where(wet > float(k), t, 0.0)
-                    d = d + ta
-                    fe = fe + ta * te_v[k, rs, ls]
-                    fn = fn + ta * tn_v[k, rs, ls]
-                    acc = [jnp.where(mi > float(k), g, ai) for mi, ai in zip(m, acc)]
-                    h, at = (2 * k) // H, (2 * k) % H
-                    moved = pltpu.roll(g, (at + 2) % H if b else at, 1) if (at + 2 * b) % H else g
-                    prof[h] = jnp.where((lane8 == at) | (lane8 == at + 1), moved, prof[h])
-                    lat_out = pn if a else ps
-                    near, far = (7, 6) if a else (0, 1)
-                    lat_out[NEAR + k : NEAR + k + 1, ls] = g[near : near + 1]
-                    lat_out[FAR + k : FAR + k + 1, ls] = g[far : far + 1]
-                if c + 1 < CHUNKS:
-                    run[0, rs, ls] = p
-                    run[1, rs, ls] = g
-                depth_out[rs, ls] = d
-                fe_out[rs, ls] = fe
-                fn_out[rs, ls] = fn
-                for i in range(8):
-                    a8[i, rs, ls] = acc[i]
-                lon_out = pe if b else pw
-                lon_out[rs, :H] = prof[0]
-                lon_out[rs, H:] = prof[1]
-    c1, c2 = 8.0 / 12.0, 1.0 / 12.0
-    fe = fe_out[...] + c1 * (beyond(a8[0], 0, -1) - beyond(a8[2], 0, 1)) - c2 * (
+    for a in range(2):
+        for b in range(2):
+            rs, ls = slice(8 * a, 8 * a + 8), slice(H * b, H * b + H)
+            m = [m8[i, rs, ls] for i in range(8)]
+            acc = [jnp.zeros((8, H), f32)] * 8
+            for k in range(K):
+                g = prefix[k, rs, ls]
+                acc = [jnp.where(mi > float(k), g, ai) for mi, ai in zip(m, acc)]
+            for i in range(8):
+                a8[i, rs, ls] = acc[i]
+    fe_out[...] = te[...] + C1 * (beyond(a8[0], 0, -1) - beyond(a8[2], 0, 1)) - C2 * (
         beyond(a8[1], 0, -2) - beyond(a8[3], 0, 2)
     )
-    fn = fn_out[...] + c1 * (beyond(a8[4], -1, 0) - beyond(a8[6], 1, 0)) - c2 * (
+    fn_out[...] = tn[...] + C1 * (beyond(a8[4], -1, 0) - beyond(a8[6], 1, 0)) - C2 * (
         beyond(a8[5], -2, 0) - beyond(a8[7], 2, 0)
     )
-    fe_out[...] = fe
-    fn_out[...] = fn
-    d = depth_out[...]
-    x = x_out[...]
-    lane_t = iota((R, H), 1)
-
-    def lon_misc(out, force, wet, dep, xs, near, far):
-        tile = out[:, H:]
-        for i, (v, at) in enumerate(((force, near), (wet, near), (wet, far), (dep, near), (dep, far), (xs, near))):
-            to = LON_MISC - H + i
-            tile = jnp.where(lane_t == to, pltpu.roll(v, (to - at) % H, 1), tile)
-        out[:, H:] = tile
-
-    lon_misc(pe, fe[:, H:], own[:, H:], d[:, H:], x[:, H:], H - 1, H - 2)
-    lon_misc(pw, fe[:, :H], own[:, :H], d[:, :H], x[:, :H], 0, 1)
-    for out, near, far in ((pn, R - 1, R - 2), (ps, 0, 1)):
-        for i, (v, at) in enumerate(((fn, near), (own, near), (own, far), (d, near), (d, far), (x, near))):
-            out[LAT_MISC + i : LAT_MISC + i + 1] = v[at : at + 1]
-
-
-def residual_kernel(fe_in, fn_in, wet, x0, depth, pe, pw, pn, ps, ge, gw, gn, gs,
-                    res, scaled, dep_x, rows_n, rows_s, pay):
+
+
+def residual_kernel(fe_in, fn_in, wet, x0, depth, pe, pw, pn, ps, lat_a, lat_b, lon_a, lon_b,
+                    res, scaled, dep_x, rows_a, rows_b, pay, ge, gw, gn, gs):
     own = wet[...]
+    la, lo = lax.axis_index("lat"), lax.axis_index("lon")
+    lat_even, lon_even = la % 2 == 0, lo % 2 == 0
+    a, b = lat_a[...], lat_b[...]
+    gn[...] = jnp.where(lat_even, a, b)
+    gs[...] = jnp.where(lat_even, b, a)
+    a, b = lon_a[...], lon_b[...]
+    ge[...] = jnp.where(lon_even, a, b)
+    gw[...] = jnp.where(lon_even, b, a)
     lane = iota((R, L), 1)
     row = iota((R, L), 0)
 
     def lon_misc(ref, i):
         return ref[:, LON_MISC + i : LON_MISC + i + 1]
-
-    la, lo = lax.axis_index("lat"), lax.axis_index("lon")
 
     def lat_misc(ref, i):
         there = la < NLAT - 1 if ref is gn else la > 0
         return jnp.where(there, ref[LAT_MISC + i : LAT_MISC + i + 1], 0.0)
 
-    def lon_pick(ref, m, col):
-        at = 2 * m.astype(jnp.int32) - 2 + col
-        return jnp.sum(jnp.where((lane == at) & (m > 0.0), ref[...], 0.0), axis=1, keepdims=True)
-
-    level = iota((FAR, L), 0).astype(f32) + 1.0
-
-    def lat_pick(ref, m, col):
-        part = ref[FAR : 2 * FAR] if col else ref[NEAR : NEAR + FAR]
-        return jnp.sum(jnp.where(level == m, part, 0.0), axis=0, keepdims=True)
+    def from_lon(ref, m, col):
+        return lon_pick(ref[...], m, col)
+
+    def from_lat(ref, m, col):
+        return lat_pick(ref[FAR : 2 * FAR] if col else ref[NEAR : NEAR + FAR], m)
 
     def cross(pick, got, sent, o1, o2, n1, n2, got_near, sent_near):
         gn_, sn_ = (0, 1) if got_near == 0 else (1, 0), (0, 1) if sent_near == 0 else (1, 0)
@@ -348,19 +391,19 @@
 
     fe = fe_in[...]
     fn = fn_in[...]
-    a, b, far_e = cross(lon_pick, ge, pe, own[:, L - 1 :], own[:, L - 2 : L - 1],
+    a, b, far_e = cross(from_lon, ge, pe, own[:, L - 1 :], own[:, L - 2 : L - 1],
                         lon_misc(ge, M_WET1), lon_misc(ge, M_WET2), 0, 1)
     fe = fe + jnp.where(lane == L - 1, a, 0.0) + jnp.where(lane == L - 2, b, 0.0)
     fe_e = lon_misc(ge, M_FORCE) + far_e
-    a, b, far_w = cross(lon_pick, gw, pw, own[:, :1], own[:, 1:2],
+    a, b, far_w = cross(from_lon, gw, pw, own[:, :1], own[:, 1:2],
                         lon_misc(gw, M_WET1), lon_misc(gw, M_WET2), 1, 0)
     fe = fe - jnp.where(lane == 0, a, 0.0) - jnp.where(lane == 1, b, 0.0)
     fe_w = lon_misc(gw, M_FORCE) - far_w
-    a, b, far_n = cross(lat_pick, gn, pn, own[R - 1 :], own[R - 2 : R - 1],
+    a, b, far_n = cross(from_lat, gn, pn, own[R - 1 :], own[R - 2 : R - 1],
                         lat_misc(gn, M_WET1), lat_misc(gn, M_WET2), 0, 0)
     fn = fn + jnp.where(row == R - 1, a, 0.0) + jnp.where(row == R - 2, b, 0.0)
     fn_n = lat_misc(gn, M_FORCE) + far_n
-    a, b, far_s = cross(lat_pick, gs, ps, own[:1], own[1:2],
+    a, b, far_s = cross(from_lat, gs, ps, own[:1], own[1:2],
                         lat_misc(gs, M_WET1), lat_misc(gs, M_WET2), 0, 0)
     fn = fn - jnp.where(row == 0, a, 0.0) - jnp.where(row == 1, b, 0.0)
     fn_s = lat_misc(gs, M_FORCE) - far_s
@@ -390,8 +433,8 @@
     s = r / diag
     res[...] = r
     scaled[...] = s
-    rows_n[...] = s[8:]
-    rows_s[...] = s[:8]
+    rows_a[...] = jnp.where(lat_even, s[8:], s[:8])
+    rows_b[...] = jnp.where(lat_even, s[:8], s[8:])
     dep_x[...] = jnp.zeros((RX, LX), f32)
     dep_x[ROWS, COLS] = d
     dep_x[7:8, COLS] = lat_misc(gs, M_DEPTH1)
@@ -420,15 +463,18 @@
             )
 
 
-def first_kernel(got, coarse, res, scaled, dep_in, sn, ss, w_out, s_x, faces, pay):
+def first_kernel(got, coarse, res, scaled, dep_in, rows_a, rows_b, w_out, s_x, faces, pay):
     la, lo = lax.axis_index("lat"), lax.axis_index("lon")
+    even = la % 2 == 0
+    a, b = rows_a[...], rows_b[...]
+    sn, ss = jnp.where(even, a, b), jnp.where(even, b, a)
     w = unpack(got[...], 0)
     w_out[...] = w
     q = coarse_rows(coarse, w)
     s = scaled[...]
     s_x[ROWS, COLS] = s
-    s_x[:8, COLS] = jnp.where(la > 0, ss[...], 0.0)
-    s_x[8 + R :, COLS] = jnp.where(la < NLAT - 1, sn[...], 0.0)
+    s_x[:8, COLS] = jnp.where(la > 0, ss, 0.0)
+    s_x[8 + R :, COLS] = jnp.where(la < NLAT - 1, sn, 0.0)
     lane = iota((R, H), 1)
     dep = dep_in[...]
     dep_x = faces.at[4]
@@ -532,20 +578,12 @@
     precond[...] = (res[...] - alpha * ad1) / face[4][own] + q2 * mask[own]
 
 
-def to_east(v):
-    return lax.ppermute(v, "lon", [(i, (i + 1) % NLON) for i in range(NLON)])
-
-
-def to_west(v):
-    return lax.ppermute(v, "lon", [((i + 1) % NLON, i) for i in range(NLON)])
-
-
-def to_north(v):
-    return lax.ppermute(v, "lat", [(i, (i + 1) % NLAT) for i in range(NLAT)])
-
-
-def to_south(v):
-    return lax.ppermute(v, "lat", [((i + 1) % NLAT, i) for i in range(NLAT)])
+def swap_a(v, axis):
+    return lax.ppermute(v, axis, [(i, i ^ 1) for i in range(16)])
+
+
+def swap_b(v, axis):
+    return lax.ppermute(v, axis, [(i, (i + 1 if i % 2 else i - 1) % 16) for i in range(16)])
 
 
 def gather(pay):
@@ -556,11 +594,11 @@
     plane, wide = (R, L), (RX, LX)
     lon_msg, lat_msg = (R, LON_LANES), (LAT_ROWS, L)
     vm = pl.BlockSpec(memory_space=pltpu.VMEM)
-    fe, fn, wet, x0, depth, pe, pw, pn, ps = pl.pallas_call(
+    prefix, te, tn, wet, x0, depth, pe, pw, pn, ps, lat_a, lat_b, lon_a, lon_b = pl.pallas_call(
         levels_kernel,
         in_specs=[pl.BlockSpec(memory_space=pl.ANY)] * 7,
-        out_specs=[vm] * 9,
-        out_shape=[in_vmem(s) for s in [plane] * 5 + [lon_msg] * 2 + [lat_msg] * 2],
+        out_specs=[vm] * 14,
+        out_shape=[in_vmem(s) for s in [(K, R, L)] + [plane] * 5 + ([lon_msg] * 2 + [lat_msg] * 2) + ([lat_msg] * 2 + [lon_msg] * 2)],
         scratch_shapes=[
             pltpu.SMEM((K,), f32),
             pltpu.VMEM(plane, jnp.int32),
@@ -569,21 +607,28 @@
             pltpu.VMEM((K, R, L), f32),
             pltpu.VMEM((K, R, L), f32),
             pltpu.VMEM((K, R, L), f32),
-            pltpu.VMEM((8, R, L), f32),
-            pltpu.VMEM((8, R, L), f32),
             pltpu.VMEM((2, R, L), f32),
+            pltpu.VMEM((2, R, H), f32),
+            pltpu.VMEM((2, FAR, L), f32),
             pltpu.SemaphoreType.DMA((3 * CHUNKS + 4,)),
         ],
         name="levels",
     )(thickness, levels, ocean_mask, eta_prev, density, tend_east, tend_north)
-    gn, gs = to_south(ps), to_north(pn)
-    ge, gw = to_west(pw), to_east(pe)
-    r0, s0, dep_x, rows_n, rows_s, pay = call(
-        residual_kernel, [plane, plane, wide, (8, L), (8, L), (NDEV, H)]
-    )(fe, fn, wet, x0, depth, pe, pw, pn, ps, ge, gw, gn, gs)
-    sn, ss = to_south(rows_s), to_north(rows_n)
+    lat_a, lat_b = swap_a(lat_a, "lat"), swap_b(lat_b, "lat")
+    lon_a, lon_b = swap_a(lon_a, "lon"), swap_b(lon_b, "lon")
+    fe, fn = call(
+        inner_kernel, [plane, plane], scratch_shapes=[pltpu.VMEM((8, R, L), f32), pltpu.VMEM((8, R, L), f32)]
+    )(prefix, wet, te, tn)
+    r0, s0, dep_x, rows_a, rows_b, pay = call(
+        residual_kernel,
+        [plane, plane, wide, (8, L), (8, L), (NDEV, H)],
+        scratch_shapes=[pltpu.VMEM(x, f32) for x in (lon_msg, lon_msg, lat_msg, lat_msg)],
+    )(fe, fn, wet, x0, depth, pe, pw, pn, ps, lat_a, lat_b, lon_a, lon_b)
+    rows_a, rows_b = swap_a(rows_a, "lat"), swap_b(rows_b, "lat")
     got = gather(pay)
-    w0, s_x, faces, pay = call(first_kernel, [G, wide, (6,) + wide, (NDEV, H)])(got, coarse, r0, s0, dep_x, sn, ss)
+    w0, s_x, faces, pay = call(first_kernel, [G, wide, (6,) + wide, (NDEV, H)])(
+        got, coarse, r0, s0, dep_x, rows_a, rows_b
+    )
     got = gather(pay)
     r1, s1, as1, x1, d0, ad0, w1, u0, net, num, pay = call(
         step_kernel, [plane] * 6 + [G, G, (3,) + G, (8, H), (NDEV, H)]

time: 83.3 us -> 81.5 us (0.978)
  starting transfers between devices: 26.4 us -> 24.4 us
    all_to_all x1, starting transfers between devices: 16.2 us -> 13.5 us  [gather(): return lax.all_to_all(pay, BOTH, 0, 0, tiled=True)]
    pallas_call x4 -> x5, Pallas kernels: 4.09 us -> 4.84 us  [run(): pl.pallas_call(kernel, out_shape=[out(s) for s in out_shapes], in_specs=[...]
  transfers between devices with their start and end apart: 7 -> 7, of which waited for: 4 -> 4; matrix products, arithmetic and copies ran while one was open for 0% -> 0% of each run, Pallas kernels for 0% -> 1%
where the time goes in v2:
time: 81.5 us; the launch traced here: 81.3 us
  blocking collectives  36.9 us (45%)
  starting transfers between devices  24.4 us (30%)
  waiting for transfers between devices  11.7 us (14%)
  Pallas kernels  7.56 us (9%)
    all_to_all x2, blocking collectives, gather(): return lax.all_to_all(pay, BOTH, 0, 0, tiled=True)  36.9 us
    all_to_all x1, starting transfers between devices, gather(): return lax.all_to_all(pay, BOTH, 0, 0, tiled=True)  13.5 us
    all_to_all x1, waiting for transfers between devices, gather(): return lax.all_to_all(pay, BOTH, 0, 0, tiled=True)  7.43 us
    ppermute x3, starting transfers between devices, swap_a(): return lax.ppermute(v, axis, [(i, i ^ 1) for i in range(16)])  6.64 us
    pallas_call x5, Pallas kernels, run(): pl.pallas_call(kernel, out_shape=[out(s) for s in out_shapes], in_specs=[...  4.84 us
    ppermute x3, starting transfers between devices, swap_b(): lax.ppermute(v, axis, [(i, (i + 1 if i % 2 else i - 1) % 16) for i in ran...  4.27 us
    ppermute x3, waiting for transfers between devices, swap_b(): lax.ppermute(v, axis, [(i, (i + 1 if i % 2 else i - 1) % 16) for i in ran...  3.47 us
    pallas_call x1, Pallas kernels, body(): pl.pallas_call(levels_kernel, in_specs=[pl.BlockSpec(memory_space=pl.ANY)...  2.72 us
  transfers between devices with their start and end apart: 7, of which 4 were waited for; matrix products, arithmetic and copies ran while one was open for 0% of the time, Pallas kernels for 1%

profile of v2, /device:TPU:1, one launch (start us, length us, event | category | flops | bytes accessed | tf_op | source)
XLA Modules:
  0.0 81.3 jit_solution(11770378014014639842)
XLA Ops:
  0.6 2.7 %levels.2 = (f32[75,16,256]{2,1,0:T(8,128)S(1)}, f32[16,256]{1,0:T(8,128)S(1)}, f32[16,256]{1,0:T(8,128)S(1)}, f32[16,256]{1,0:T(8,128)S(1)}, f32[16,256]{1,0:T(...) custom-call(f32[75]{0:T(128)} %thick.1, ...), custom_call_target="tpu_custom_call" | custom-call | tf_op jit(solution)/shard_map/levels/pallas_call | solution.py:597
  3.4 0.0 copy-start
  3.4 3.3 %collective-permute-start = (f32[168,256]{1,0:T(8,128)S(1)}, f32[168,256]{1,0:T(8,128)S(1)}, u32[]{:S(2)}, u32[]{:S(2)}) collective-permute-start(f32[168,256]{1,0:T(8,128)S(1)} %get-tuple-element.51), channel_id=1, source_target_pairs={{0,16},{16,0},{32,48},{48,32},{64,80},{80,64},{96,112},{112,96},{1... | collective-permute-start | bytes 516104 | tf_op jit(solution)/shard_map/ppermute | solution.py:582
  6.7 0.0 collective-permute-start.1
  6.7 1.1 %collective-permute-start.2 = (f32[16,256]{1,0:T(8,128)S(1)}, f32[16,256]{1,0:T(8,128)S(1)}, u32[]{:S(2)}, u32[]{:S(2)}) collective-permute-start(f32[16,256]{1,0:T(8,128)S(1)} %get-tuple-element.53), channel_id=1, source_target_pairs={{0,1},{1,0},{2,3},{3,2},{4,5},{5,4},{6,7},{7,6},{8,9},{9,8},{10,11... | collective-permute-start | bytes 49160 | tf_op jit(solution)/shard_map/ppermute | solution.py:582
  7.8 4.3 %collective-permute-start.3 = (f32[16,256]{1,0:T(8,128)S(1)}, f32[16,256]{1,0:T(8,128)S(1)}, u32[]{:S(2)}, u32[]{:S(2)}) collective-permute-start(f32[16,256]{1,0:T(8,128)S(1)} %get-tuple-element.54), channel_id=1, source_target_pairs={{0,15},{1,2},{2,1},{3,4},{4,3},{5,6},{6,5},{7,8},{8,7},{9,10},{10,... | collective-permute-start | bytes 49160 | tf_op jit(solution)/shard_map/ppermute | solution.py:586
  12.1 0.7 shard_map.95
  12.8 0.0 collective-permute-done.2.lon_a
  12.8 0.9 %collective-permute-done.3.lon_b = f32[16,256]{1,0:T(8,128)S(1)} collective-permute-done((f32[16,256]{1,0:T(8,128)S(1)}, f32[16,256]{1,0:T(8,128)S(1)}, u32[]{:S(2)}, u32[]{:S(2)}) %collective-permute-start.3) | collective-permute-done | bytes 16416 | tf_op jit(solution)/shard_map/ppermute | solution.py:586
  13.7 0.0 collective-permute-done.lat_a
  13.7 0.0 collective-permute-done.1.lat_b
  13.7 1.3 %shard_map.96 = (f32[16,256]{1,0:T(8,128)S(1)}, f32[16,256]{1,0:T(8,128)S(1)}, f32[32,512]{1,0:T(8,128)S(1)}, f32[8,256]{1,0:T(8,128)S(1)}, f32[8,256]{1,0:T(8,128)S(1)}, /*index=5*/f32[256,128]{1,0:T(8,128)}) custom-call(f32[16,256]{1,0:T(8,128)S(1)} %get-tuple-element.43.fe_in, f32[16,256]{1,0:T(8,128)S(1)} %get-tuple-element.44.fn_in, ...), custom_call_target="tpu_custom_call" | custom-call | tf_op jit(solution)/shard_map/pallas_call | solution.py:33
  15.0 13.5 %all-to-all-start = ((f32[256,1,128]{2,1,0:T(1,128)}), f32[256,1,128]{2,1,0:T(1,128)S(1)}, u32[]{:S(2)}, u32[]{:S(2)}) async-start(f32[256,1,128]{2,1,0:T(1,128)} %bitcast.1), calls=%async_computation | async-start | bytes 262144 | tf_op jit(solution)/shard_map/all_to_all | solution.py:590
  28.6 2.2 %collective-permute-start.4 = (f32[8,256]{1,0:T(8,128)S(1)}, f32[8,256]{1,0:T(8,128)S(1)}, u32[]{:S(2)}, u32[]{:S(2)}) collective-permute-start(f32[8,256]{1,0:T(8,128)S(1)} %get-tuple-element.59), channel_id=1, source_target_pairs={{0,16},{16,0},{32,48},{48,32},{64,80},{80,64},{96,112},{112,96},{1... | collective-permute-start | bytes 24584 | tf_op jit(solution)/shard_map/ppermute | solution.py:582
  30.8 0.0 collective-permute-start.5
  30.8 0.8 %collective-permute-done.4.rows_a = f32[8,256]{1,0:T(8,128)S(1)} collective-permute-done((f32[8,256]{1,0:T(8,128)S(1)}, f32[8,256]{1,0:T(8,128)S(1)}, u32[]{:S(2)}, u32[]{:S(2)}) %collective-permute-start.4) | collective-permute-done | bytes 8224 | tf_op jit(solution)/shard_map/ppermute | solution.py:582
  31.6 2.6 %collective-permute-done.5.rows_b = f32[8,256]{1,0:T(8,128)S(1)} collective-permute-done((f32[8,256]{1,0:T(8,128)S(1)}, f32[8,256]{1,0:T(8,128)S(1)}, u32[]{:S(2)}, u32[]{:S(2)}) %collective-permute-start.5) | collective-permute-done | bytes 8224 | tf_op jit(solution)/shard_map/ppermute | solution.py:586
  34.2 7.4 %all-to-all-done = f32[256,1,128]{2,1,0:T(1,128)S(1)} async-done(((f32[256,1,128]{2,1,0:T(1,128)}), f32[256,1,128]{2,1,0:T(1,128)S(1)}, u32[]{:S(2)}, u32[]{:S(2)}) %all-to-all-start) | async-done | bytes 131104 | tf_op jit(solution)/shard_map/all_to_all | solution.py:590
  41.6 0.0 copy-done
  41.6 0.4 shard_map.97
  42.1 18.4 %all_to_all.33 = f32[256,1,128]{2,1,0:T(1,128)S(1)} all-to-all(f32[256,1,128]{2,1,0:T(1,128)S(1)} %bitcast.16), channel_id=1, replica_groups=mesh['lat'=16,'lon'=16] {'lat','lon'}, dimensions={0} | all-to-all | bytes 262144 | tf_op jit(solution)/shard_map/all_to_all | solution.py:590
  60.5 0.9 %shard_map.98 = (f32[16,256]{1,0:T(8,128)S(1)}, f32[16,256]{1,0:T(8,128)S(1)}, f32[16,256]{1,0:T(8,128)S(1)}, f32[16,256]{1,0:T(8,128)S(1)}, f32[16,256]{1,0:T(8...) custom-call(f32[256,128]{1,0:T(8,128)S(1)} %bitcast.12, ...), custom_call_target="tpu_custom_call" | custom-call | tf_op jit(solution)/shard_map/pallas_call | solution.py:33
  61.4 18.4 %all_to_all.34 = f32[256,1,128]{2,1,0:T(1,128)S(1)} all-to-all(f32[256,1,128]{2,1,0:T(1,128)S(1)} %bitcast.15), channel_id=1, replica_groups=mesh['lat'=16,'lon'=16] {'lat','lon'}, dimensions={0} | all-to-all | bytes 262144 | tf_op jit(solution)/shard_map/all_to_all | solution.py:590
  79.8 1.5 %shard_map.99 = (f32[16,256]{1,0:T(8,128)}, f32[16,256]{1,0:T(8,128)}) custom-call(f32[256,128]{1,0:T(8,128)S(1)} %bitcast.14, f32[32,128]{1,0:T(8,128)S(1)} %get-tuple-element.66.w_in, f32[32,128]{1,0:T(8,128)S(1)} %get-tuple-element.67.u_in, f32[3,32,128]{2,1,0:T(8,128)S(1)} %get-tuple-element.68.net, f32[8,128]{1,0:T(8,128)S(1)} %get-tuple-element.69.num, ...), custom_call_target="tpu_custom_call" | custom-call | tf_op jit(solution)/shard_map/pallas_call | solution.py:33
Async XLA Ops:
  3.4 38.3 %copy-start = (f32[16,4096]{1,0:T(8,128)S(1)}, f32[16,4096]{1,0:T(8,128)}, u32[]{:S(2)}) copy-start(f32[16,4096]{1,0:T(8,128)} %coarse.5) | copy-start | bytes 786436
  3.4 10.3 %collective-permute-start = (f32[168,256]{1,0:T(8,128)S(1)}, f32[168,256]{1,0:T(8,128)S(1)}, u32[]{:S(2)}, u32[]{:S(2)}) collective-permute-start(f32[168,256]{1,0:T(8,128)S(1)} %get-tuple-element.51), channel_id=1, source_target_pairs={{0,16},{16,0},{32,48},{48,32},{64,80},{80,64},{96,112},{112,96},{1... | collective-permute-start | bytes 516104 | tf_op jit(solution)/shard_map/ppermute | solution.py:582
  6.7 7.0 %collective-permute-start.1 = (f32[168,256]{1,0:T(8,128)S(1)}, f32[168,256]{1,0:T(8,128)S(1)}, u32[]{:S(2)}, u32[]{:S(2)}) collective-permute-start(f32[168,256]{1,0:T(8,128)S(1)} %get-tuple-element.52), channel_id=1, source_target_pairs={{0,240},{16,32},{32,16},{48,64},{64,48},{80,96},{96,80},{112,128},... | collective-permute-start | bytes 516104 | tf_op jit(solution)/shard_map/ppermute | solution.py:586
  6.7 6.1 %collective-permute-start.2 = (f32[16,256]{1,0:T(8,128)S(1)}, f32[16,256]{1,0:T(8,128)S(1)}, u32[]{:S(2)}, u32[]{:S(2)}) collective-permute-start(f32[16,256]{1,0:T(8,128)S(1)} %get-tuple-element.53), channel_id=1, source_target_pairs={{0,1},{1,0},{2,3},{3,2},{4,5},{5,4},{6,7},{7,6},{8,9},{9,8},{10,11... | collective-permute-start | bytes 49160 | tf_op jit(solution)/shard_map/ppermute | solution.py:582
  7.8 5.9 %collective-permute-start.3 = (f32[16,256]{1,0:T(8,128)S(1)}, f32[16,256]{1,0:T(8,128)S(1)}, u32[]{:S(2)}, u32[]{:S(2)}) collective-permute-start(f32[16,256]{1,0:T(8,128)S(1)} %get-tuple-element.54), channel_id=1, source_target_pairs={{0,15},{1,2},{2,1},{3,4},{4,3},{5,6},{6,5},{7,8},{8,7},{9,10},{10,... | collective-permute-start | bytes 49160 | tf_op jit(solution)/shard_map/ppermute | solution.py:586
  15.0 26.6 %all-to-all-start = ((f32[256,1,128]{2,1,0:T(1,128)}), f32[256,1,128]{2,1,0:T(1,128)S(1)}, u32[]{:S(2)}, u32[]{:S(2)}) async-start(f32[256,1,128]{2,1,0:T(1,128)} %bitcast.1), calls=%async_computation | async-start | bytes 262144 | tf_op jit(solution)/shard_map/all_to_all | solution.py:590
  28.6 3.1 %collective-permute-start.4 = (f32[8,256]{1,0:T(8,128)S(1)}, f32[8,256]{1,0:T(8,128)S(1)}, u32[]{:S(2)}, u32[]{:S(2)}) collective-permute-start(f32[8,256]{1,0:T(8,128)S(1)} %get-tuple-element.59), channel_id=1, source_target_pairs={{0,16},{16,0},{32,48},{48,32},{64,80},{80,64},{96,112},{112,96},{1... | collective-permute-start | bytes 24584 | tf_op jit(solution)/shard_map/ppermute | solution.py:582
  30.8 3.4 %collective-permute-start.5 = (f32[8,256]{1,0:T(8,128)S(1)}, f32[8,256]{1,0:T(8,128)S(1)}, u32[]{:S(2)}, u32[]{:S(2)}) collective-permute-start(f32[8,256]{1,0:T(8,128)S(1)} %get-tuple-element.60), channel_id=1, source_target_pairs={{0,240},{16,32},{32,16},{48,64},{64,48},{80,96},{96,80},{112,128},... | collective-permute-start | bytes 24584 | tf_op jit(solution)/shard_map/ppermute | solution.py:586
